TPU v7x, 32 devices: a whole 2x2x4 slice. The times are simulated.
32 devices in a mesh: wide: 8 (over z, y), narrow: 4 (over x, core).
Axes of the slice: x: 2, y: 2, z: 4, core: 2. Of those that a mesh axis runs over, the one named last changes fastest.
Arguments:
- inputs: bfloat16 [16384, 1024], P('wide', 'narrow'), may hold values from -6 to 6
- lengths: int32 [16], P('wide'), may hold values from 256 to 1024, as said below
- attn_gain: float32 [1024], replicated, may hold values from 0.25 to 1.75
- attn_in_weight: bfloat16 [3, 1024, 1024], P(None, 'wide', 'narrow'), may hold values from -0.1875 to 0.1875
- attn_out_weight: bfloat16 [1024, 1024], P('narrow', 'wide'), may hold values from -3 to 3
- mlp_gain: float32 [1024], replicated, may hold values from 0.25 to 1.75
- mlp_in_weight: bfloat16 [2, 1024, 2624], P(None, 'wide', 'narrow'), may hold values from -0.1875 to 0.1875
- mlp_out_weight: bfloat16 [2624, 1024], P('narrow', 'wide'), may hold values from -0.125 to 0.125
- cotangent: bfloat16 [16384, 1024], P('wide', 'narrow'), may hold values from -6 to 6
Outputs:
- output: float32 [16384, 1024], P('wide', 'narrow')
- inputs_grad: float32 [16384, 1024], P('wide', 'narrow')
- attn_gain_grad: float32 [1024], P('narrow')
- attn_in_grad: float32 [3, 1024, 1024], P(None, 'wide', 'narrow')
- attn_out_grad: float32 [1024, 1024], P('narrow', 'wide')
- mlp_gain_grad: float32 [1024], P('narrow')
- mlp_in_grad: float32 [2, 1024, 2624], P(None, 'wide', 'narrow')
- mlp_out_grad: float32 [2624, 1024], P('narrow', 'wide')
Inputs may be any that keep to these rules, and one draw needn't show every extreme that they name: `lengths`: each sequence's live slots; its slots from there on are padding; some sequence has all 1024 live.
All inputs are finite; a program needn't handle non-finite values.
Results may differ from a plain program's by a relative error of at most 0.02.
Values may be sent and summed in bfloat16 or wider, within the bound.
No kernel may reach another device: no remote copies, remote signals or barrier semaphores. Data moves between devices by JAX's collectives and lax.ppermute only.
A program may use at most 128 MiB of HBM per device.

v0:
```python
import functools

import jax
import jax.numpy as jnp
from jax import lax
from jax.experimental import pallas as pl
from jax.experimental.pallas import tpu as pltpu
from jax.sharding import PartitionSpec as P


HEAD_DIM = 64
epsilon = 1e-05
theta_base = 160000.0
masked_score = -1e30
BLOCK = 256
GLUE = 512
TAIL = 16
STAT_ROWS = 8
f32 = jnp.float32
bf16 = jnp.bfloat16


def dot_nn(left, right):
    return lax.dot_general(left, right, (((1,), (0,)), ((), ())), preferred_element_type=f32)


def dot_nt(left, right):
    return lax.dot_general(left, right, (((1,), (1,)), ((), ())), preferred_element_type=f32)


def dot_tn(left, right):
    return lax.dot_general(left, right, (((0,), (0,)), ((), ())), preferred_element_type=f32)


def block_rows(index):
    return pl.ds(pl.multiple_of(index * BLOCK, BLOCK), BLOCK)


def feature_block(index, distance, width):
    return pl.ds(pl.multiple_of((index ^ distance) * width, width), width)


def norm_parts(parts, full):
    mean = sum(jnp.sum(part, axis=-1, keepdims=True) for part in parts) / full
    parts = [part - mean for part in parts]
    spread = sum(jnp.sum(part * part, axis=-1, keepdims=True) for part in parts) / full
    factor = lax.rsqrt(spread + epsilon)
    return [part * factor for part in parts], mean, factor


def columns_to_rows(columns):
    lane = lax.broadcasted_iota(jnp.int32, (BLOCK, 128), 1)
    packed = jnp.zeros((BLOCK, 128), f32)
    for place, column in enumerate(columns):
        packed = jnp.where(lane == place, column, packed)
    return packed.T[0:STAT_ROWS, :]


def turn(values, cos_ref, low_ref, high_ref, rows, sign):
    parts = []
    for start in range(0, values.shape[1], 128):
        part = values[:, start : start + 128]
        swapped = pltpu.roll(part, 96, 1) * low_ref[rows, :] + pltpu.roll(part, 32, 1) * high_ref[
            rows, :
        ]
        parts.append(part * cos_ref[rows, :] + sign * swapped)
    return jnp.concatenate(parts, axis=1)


def head_only(values, head):
    lane = lax.broadcasted_iota(jnp.int32, values.shape, 1)
    inside = (lane >= head * HEAD_DIM) & (lane < (head + 1) * HEAD_DIM)
    return jnp.where(inside, values.astype(f32), 0.0).astype(bf16)


def send_tail(send, slots, first, second):
    lanes = send.shape[1]
    pieces = [row[:, start : start + lanes] for row in (first, second) for start in range(0, slots, lanes)]
    if len(pieces) < TAIL:
        pieces.append(jnp.zeros((TAIL - len(pieces), lanes), f32))
    send[slots : slots + TAIL, :] = jnp.concatenate(pieces, axis=0).astype(bf16)


def attend_kernel(place_ref, lengths, *refs, seq, count, width, heads, slots, full):
    pieces = refs[:count]
    gain, weight, cos_ref, low_ref, high_ref = refs[count : count + 5]
    normed, q_out, k_out, v_out, attended, log_sum, stats, keep, send = refs[count + 5 : count + 14]
    values_t, out_t = refs[count + 14 :]
    index = place_ref[0]
    length = lengths[seq]
    live = pl.cdiv(length, BLOCK)
    blocks = slots // BLOCK

    def project(block, carry):
        rows = block_rows(block)
        units, mean, factor = norm_parts([piece[rows, :].astype(f32) for piece in pieces], full)
        for place, unit in enumerate(units):
            gained = unit * gain[pl.ds(index ^ place, 1), :]
            normed[rows, feature_block(index, place, width)] = gained.astype(bf16)
        stats[:, rows] = columns_to_rows((mean, factor))
        row = normed[rows, :]
        turned = turn(dot_nn(row, weight[0]), cos_ref, low_ref, high_ref, rows, 1.0)
        q_out[rows, :] = (turned.astype(bf16).astype(f32) * HEAD_DIM**-0.5).astype(bf16)
        turned = turn(dot_nn(row, weight[1]), cos_ref, low_ref, high_ref, rows, 1.0)
        k_out[rows, :] = turned.astype(bf16)
        v_out[rows, :] = dot_nn(row, weight[2]).astype(bf16)
        return carry

    def clear(block, carry):
        rows = block_rows(block)
        normed[rows, :] = jnp.zeros((BLOCK, full), bf16)
        for ref in (q_out, k_out, v_out, attended):
            ref[rows, :] = jnp.zeros((BLOCK, width), bf16)
        stats[:, rows] = jnp.zeros((STAT_ROWS, BLOCK), f32)
        keep[rows, :] = jnp.zeros((BLOCK, keep.shape[1]), bf16)
        send[rows, :] = jnp.zeros((BLOCK, send.shape[1]), bf16)
        return carry

    lax.fori_loop(0, live, project, 0)
    lax.fori_loop(live, blocks, clear, 0)
    log_sum[...] = jnp.zeros(log_sum.shape, f32)

    def attend(count_live):
        span = count_live * BLOCK
        values_t[:, 0:span] = v_out[0:span, :].T

        def query_block(block, carry):
            rows = block_rows(block)
            queries = q_out[rows, :]
            for head in range(heads):
                mine = slice(head * HEAD_DIM, (head + 1) * HEAD_DIM)
                scores = dot_nt(k_out[0:span, :], head_only(queries, head))
                slot = lax.broadcasted_iota(jnp.int32, (span, BLOCK), 0)
                scores = jnp.where(slot < length, scores, masked_score)
                top = jnp.max(scores, axis=0, keepdims=True)
                weights = jnp.exp(scores - top)
                total = jnp.sum(weights, axis=0, keepdims=True)
                result = dot_nn(values_t[mine, 0:span], weights.astype(bf16))
                out_t[mine, :] = result * (1.0 / total)
                log_sum[head : head + 1, rows] = top + jnp.log(total)
            attended[rows, :] = out_t[...].T.astype(bf16)
            return carry

        lax.fori_loop(0, count_live, query_block, 0)

    for count_live in range(1, blocks + 1):
        pl.when(live == count_live)(functools.partial(attend, count_live))

    def output(block, carry):
        rows = block_rows(block)
        row = attended[rows, :]
        for place in range(count):
            part = dot_nt(row, weight[3, feature_block(index, place, width), :])
            target = slice((place // 2) * width, (place // 2 + 1) * width)
            if place % 2:
                send[rows, target] = part.astype(bf16)
            else:
                keep[rows, target] = part.astype(bf16)
        return carry

    lax.fori_loop(0, live, output, 0)


def mlp_kernel(place_ref, lengths, *refs, seq, count, width, slots, full):
    rows_in = refs[:count]
    grads_in = refs[count : 2 * count]
    gain, weight = refs[2 * count : 2 * count + 2]
    (normed, grads, mixed, grad_expanded, stats, out_keep, out_send, back_keep, back_send, kept) = (
        refs[2 * count + 2 :]
    )
    index = place_ref[0]
    length = lengths[seq]
    block = pl.program_id(0)
    rows = block_rows(block)

    @pl.when(block * BLOCK < length)
    def _():
        slot = block * BLOCK + lax.broadcasted_iota(jnp.int32, (BLOCK, 1), 0)
        units, mean, factor = norm_parts([piece[...].astype(f32) for piece in rows_in], full)
        for place, unit in enumerate(units):
            here = feature_block(index, place, width)
            gained = unit * gain[pl.ds(index ^ place, 1), :]
            normed[:, here] = gained.astype(bf16)
            grad = jnp.where(slot < length, grads_in[place][...].astype(f32), 0.0)
            grads[:, here] = grad.astype(bf16)
        row = normed[...]
        grad = grads[...]
        gate = dot_nn(row, weight[0])
        linear = dot_nn(row, weight[1])
        grad_mixed = dot_nn(grad, weight[2])
        phi = 0.5 + 0.5 * lax.erf(gate * (0.5**0.5))
        activated = gate * phi
        density = jnp.exp(-0.5 * gate * gate) * (0.5 / jnp.pi) ** 0.5
        mixed_low = (activated * linear).astype(bf16)
        mixed[...] = mixed_low
        first = (grad_mixed * linear * (phi + gate * density)).astype(bf16)
        second = (grad_mixed * activated).astype(bf16)
        grad_expanded[0] = first
        grad_expanded[1] = second
        plain_sum = jnp.zeros((BLOCK, 1), f32)
        unit_sum = jnp.zeros((BLOCK, 1), f32)
        for place in range(count):
            here = feature_block(index, place, width)
            target = slice((place // 2) * width, (place // 2 + 1) * width)
            part = dot_nt(mixed_low, weight[2, here, :])
            back = dot_nt(first, weight[0, here, :]) + dot_nt(second, weight[1, here, :])
            plain_sum += jnp.sum(back * gain[pl.ds(index ^ place, 1), :], axis=-1, keepdims=True)
            unit_sum += jnp.sum(back * normed[:, here].astype(f32), axis=-1, keepdims=True)
            if place % 2:
                out_send[:, target] = part.astype(bf16)
                back_send[rows, target] = back.astype(bf16)
            else:
                out_keep[:, target] = part.astype(bf16)
                back_keep[:, target] = back.astype(bf16)
        lines = columns_to_rows((mean, factor, plain_sum, unit_sum))
        stats[...] = lines
        kept[:, rows] = lines

    @pl.when(block * BLOCK >= length)
    def _():
        for ref in (normed, grads, mixed, out_keep, out_send, back_keep, grad_expanded, stats):
            ref[...] = jnp.zeros(ref.shape, ref.dtype)
        back_send[rows, :] = jnp.zeros((BLOCK, back_send.shape[1]), bf16)
        kept[:, rows] = jnp.zeros((STAT_ROWS, BLOCK), f32)

    @pl.when(block == pl.num_programs(0) - 1)
    def _():
        send_tail(back_send, slots, kept[2:3, :], kept[3:4, :])


def attend_back_kernel(place_ref, lengths, *refs, seq, count, width, heads, slots, full):
    grads_in = refs[:count]
    (q_in, k_in, v_in, attended, log_sum, normed, gain, weight, cos_ref, low_ref, high_ref) = refs[
        count : count + 11
    ]
    grads, grad_projected, stats, keep, send = refs[count + 11 : count + 16]
    (grad_att, delta, keys_t, probs_all, scores_all, query_t, key_total, value_total) = refs[
        count + 16 :
    ]
    index = place_ref[0]
    length = lengths[seq]
    live = pl.cdiv(length, BLOCK)
    blocks = slots // BLOCK

    def enter(block, carry):
        rows = block_rows(block)
        for place in range(count):
            grads[rows, feature_block(index, place, width)] = grads_in[place][rows, :]
        grad = dot_nn(grads[rows, :], weight[3]).astype(bf16)
        grad_att[rows, :] = grad
        inner = (grad.astype(f32) * attended[rows, :].astype(f32)).T
        for head in range(heads):
            mine = slice(head * HEAD_DIM, (head + 1) * HEAD_DIM)
            delta[head : head + 1, rows] = jnp.sum(inner[mine, :], axis=0, keepdims=True)
        return carry

    def clear(block, carry):
        rows = block_rows(block)
        grads[rows, :] = jnp.zeros((BLOCK, full), bf16)
        for place in range(3):
            grad_projected[place, rows, :] = jnp.zeros((BLOCK, width), bf16)
        stats[:, rows] = jnp.zeros((STAT_ROWS, BLOCK), f32)
        keep[rows, :] = jnp.zeros((BLOCK, keep.shape[1]), bf16)
        send[rows, :] = jnp.zeros((BLOCK, send.shape[1]), bf16)
        return carry

    lax.fori_loop(0, live, enter, 0)
    lax.fori_loop(live, blocks, clear, 0)

    def attend(count_live):
        span = count_live * BLOCK
        keys_t[:, 0:span] = k_in[0:span, :].T
        key_total[0:span, :] = jnp.zeros((span, width), f32)
        value_total[0:span, :] = jnp.zeros((span, width), f32)

        def query_block(block, carry):
            rows = block_rows(block)
            queries = [head_only(q_in[rows, :], head) for head in range(heads)]
            grad_rows = [head_only(grad_att[rows, :], head) for head in range(heads)]
            for head in range(heads):
                mine = slice(head * HEAD_DIM, (head + 1) * HEAD_DIM)
                lanes = slice(head * BLOCK, (head + 1) * BLOCK)
                scores = dot_nt(k_in[0:span, :], queries[head])
                slot = lax.broadcasted_iota(jnp.int32, (span, BLOCK), 0)
                scores = jnp.where(slot < length, scores, masked_score)
                weights = jnp.exp(scores - log_sum[head : head + 1, rows])
                grad_weights = dot_nt(v_in[0:span, :], grad_rows[head])
                grad_scores = (weights * (grad_weights - delta[head : head + 1, rows])).astype(bf16)
                probs_all[0:span, lanes] = weights.astype(bf16)
                scores_all[0:span, lanes] = grad_scores
                query_t[mine, :] = dot_nn(keys_t[mine, 0:span], grad_scores)
            value_total[0:span, :] += dot_nn(probs_all[0:span, :], jnp.concatenate(grad_rows, axis=0))
            key_total[0:span, :] += dot_nn(scores_all[0:span, :], jnp.concatenate(queries, axis=0))
            turned = turn(query_t[...].T * HEAD_DIM**-0.5, cos_ref, low_ref, high_ref, rows, -1.0)
            grad_projected[0, rows, :] = turned.astype(bf16)
            return carry

        lax.fori_loop(0, count_live, query_block, 0)

    for count_live in range(1, blocks + 1):
        pl.when(live == count_live)(functools.partial(attend, count_live))

    def leave(block, carry):
        rows = block_rows(block)
        turned = turn(key_total[rows, :], cos_ref, low_ref, high_ref, rows, -1.0)
        grad_projected[1, rows, :] = turned.astype(bf16)
        grad_projected[2, rows, :] = value_total[rows, :].astype(bf16)
        plain_sum = jnp.zeros((BLOCK, 1), f32)
        unit_sum = jnp.zeros((BLOCK, 1), f32)
        for place in range(count):
            here = feature_block(index, place, width)
            target = slice((place // 2) * width, (place // 2 + 1) * width)
            back = sum(
                dot_nt(grad_projected[kind, rows, :], weight[kind, here, :]) for kind in range(3)
            )
            plain_sum += jnp.sum(back * gain[pl.ds(index ^ place, 1), :], axis=-1, keepdims=True)
            unit_sum += jnp.sum(back * normed[rows, here].astype(f32), axis=-1, keepdims=True)
            if place % 2:
                send[rows, target] = back.astype(bf16)
            else:
                keep[rows, target] = back.astype(bf16)
        zero = jnp.zeros((BLOCK, 1), f32)
        stats[:, rows] = columns_to_rows((zero, zero, plain_sum, unit_sum))
        return carry

    lax.fori_loop(0, live, leave, 0)
    send_tail(send, slots, stats[2:3, :], stats[3:4, :])


def rows_to_columns(rows):
    filler = jnp.zeros((128 - len(rows), rows[0].shape[1]), f32)
    return jnp.concatenate([*rows, filler], axis=0).T


def read_tail(tail, slots):
    values = tail[...].astype(f32)
    lanes = values.shape[1]
    lines = slots // lanes
    return [
        jnp.concatenate([values[row : row + 1] for row in range(start, start + lines)], axis=1)
        for start in (0, lines)
    ]


def near_kernel(*refs, blocks, terms, width, slots, tailed):
    parts = refs[: blocks * terms]
    going = refs[blocks * terms + 2 * tailed]
    step = pl.program_id(0)
    here = pl.ds(pl.multiple_of(step * GLUE, GLUE), GLUE)
    for block in range(blocks):
        total = sum(ref[...].astype(f32) for ref in parts[block * terms : (block + 1) * terms])
        going[here, block * width : (block + 1) * width] = total.astype(bf16)
    if tailed:
        tail, sums = refs[blocks * terms : blocks * terms + 2]
        sums_out = refs[-1]

        @pl.when(step == 0)
        def _():
            plain, unit = read_tail(tail, slots)
            plain = plain + sums[2:3, :]
            unit = unit + sums[3:4, :]
            empty = jnp.zeros((2, slots), f32)
            sums_out[...] = jnp.concatenate([empty, plain, unit, empty, empty], axis=0)
            send_tail(going, slots, plain, unit)


def residual_kernel(inputs, *refs):
    *terms, out, low = refs
    total = inputs[...].astype(f32) + sum(term[...].astype(f32) for term in terms)
    out[...] = total
    low[...] = total.astype(bf16)


def output_kernel(place_ref, lengths, residual, *refs, seq, terms):
    out = refs[-1]
    slot = pl.program_id(0) * GLUE + lax.broadcasted_iota(jnp.int32, (GLUE, 1), 0)
    total = residual[...] + sum(term[...].astype(f32) for term in refs[:terms])
    out[...] = jnp.where(slot < lengths[seq], total, 0.0)


def norm_back_kernel(place_ref, lengths, *refs, seq, terms, slots, full, masked):
    parts = refs[:terms]
    (tail, sums, stats, source, base, gain) = refs[terms : terms + 6]
    low = refs[-2] if masked else None
    out = refs[-3] if masked else refs[-2]
    gain_grad = refs[-1]
    step = pl.program_id(0)
    plain, unit_sum = read_tail(tail, slots)
    here = pl.ds(pl.multiple_of(step * GLUE, GLUE), GLUE)
    columns = rows_to_columns([stats[0:1, here], stats[1:2, here], sums[2:3, here], sums[3:4, here]])
    lane_block = [plain[:, start : start + GLUE] for start in range(0, slots, GLUE)]
    unit_block = [unit_sum[:, start : start + GLUE] for start in range(0, slots, GLUE)]
    more_plain = lane_block[0]
    more_unit = unit_block[0]
    for place in range(1, len(lane_block)):
        more_plain = jnp.where(step == place, lane_block[place], more_plain)
        more_unit = jnp.where(step == place, unit_block[place], more_unit)
    more = rows_to_columns([more_plain, more_unit])
    mean, factor = columns[:, 0:1], columns[:, 1:2]
    plain_mean = (columns[:, 2:3] + more[:, 0:1]) / full
    unit_mean = (columns[:, 3:4] + more[:, 1:2]) / full
    unit = (source[...].astype(f32) - mean) * factor
    gradient = sum(part[...].astype(f32) for part in parts)
    inner = gradient * gain[pl.ds(place_ref[0], 1), :] - plain_mean - unit * unit_mean
    below = base[...].astype(f32)
    if masked:
        slot = step * GLUE + lax.broadcasted_iota(jnp.int32, (GLUE, 1), 0)
        below = jnp.where(slot < lengths[seq], below, 0.0)
    total = below + factor * inner
    out[...] = total
    if masked:
        low[...] = total.astype(bf16)

    @pl.when(step == 0)
    def _():
        gain_grad[...] = jnp.zeros(gain_grad.shape, f32)

    gain_grad[0:1, :] += jnp.sum(gradient * unit, axis=0, keepdims=True)


def grad_kernel(*refs, pairs, seq_count):
    out = refs[-1]
    place = 0
    cursor = 0
    for kinds in pairs:
        lefts = refs[cursor : cursor + seq_count]
        rights = refs[cursor + seq_count : cursor + 2 * seq_count]
        cursor += 2 * seq_count
        for kind in range(kinds):
            total = sum(dot_tn(left[...], right[kind]) for left, right in zip(lefts, rights))
            for step in range(out.shape[0]):
                rows = out.shape[2]
                out[step, place] = total[step * rows : (step + 1) * rows, :].astype(bf16)
            place += 1


def weight_grads(groups, wide_count, full, micros, earlier):
    rows = full // wide_count
    per_step = max(BLOCK // rows, 1)
    columns = groups[0][1][0].shape[2]
    slots = groups[0][0][0].shape[0]
    seq_count = len(groups[0][0])
    pairs = tuple(rights[0].shape[0] for _, rights in groups)
    operands = []
    specs = []
    for lefts, rights in groups:
        for left in lefts:
            operands.append(left)
            specs.append(pl.BlockSpec((slots, rows * per_step), lambda step: (0, step)))
        for right in rights:
            operands.append(right)
            specs.append(pl.BlockSpec(right.shape, lambda step: (0, 0, 0)))
    kinds = sum(pairs)
    body = functools.partial(grad_kernel, pairs=pairs, seq_count=seq_count)
    body, operands, specs = after(body, operands, specs, earlier, 0)
    return pl.pallas_call(
        body,
        grid=(wide_count // per_step,),
        in_specs=specs,
        out_specs=pl.BlockSpec((per_step, kinds, rows, columns), lambda step: (step, 0, 0, 0)),
        out_shape=jax.ShapeDtypeStruct((wide_count, kinds, rows, columns), bf16),
        cost_estimate=estimate(micros),
    )(*operands)


def whole(shape):
    return pl.BlockSpec(shape, lambda step, *scalars: (0,) * len(shape))


def striped(columns, seq=0, blocks=0, column=0, rows=GLUE):
    return pl.BlockSpec((rows, columns), lambda step, *scalars: (seq * blocks + step, column))


def tail_spec(columns, slots):
    return pl.BlockSpec((TAIL, columns), lambda step, *scalars: (slots // TAIL, 0))


def after(body, operands, specs, earlier, scalars):
    place = scalars + len(operands)

    def ordered(*refs):
        return body(*refs[:place], *refs[place + len(earlier) :])

    unread = [pl.BlockSpec(memory_space=pl.ANY)] * len(earlier)
    return ordered, [*operands, *earlier], [*specs, *unread]


def estimate(micros):
    return pl.CostEstimate(flops=int(micros * 1e9), transcendentals=0, bytes_accessed=1 << 20)


def glue_call(body, scalars, operands, specs, outs, out_specs, steps, aliases=()):
    return pl.pallas_call(
        body,
        grid_spec=pltpu.PrefetchScalarGridSpec(
            num_scalar_prefetch=len(scalars), grid=(steps,), in_specs=specs, out_specs=out_specs
        ),
        out_shape=[jax.ShapeDtypeStruct(shape, kind) for shape, kind in outs],
        input_output_aliases=dict(aliases),
        cost_estimate=estimate(2),
    )(*scalars, *operands)


def call_kernel(
    body, meta, operands, specs, outs, scratch, micros, earlier, steps=1, out_specs=None
):
    body, operands, specs = after(body, operands, specs, earlier, 2)
    return pl.pallas_call(
        body,
        grid_spec=pltpu.PrefetchScalarGridSpec(
            num_scalar_prefetch=2,
            grid=(steps,),
            in_specs=specs,
            out_specs=out_specs or [whole(shape) for shape, _ in outs],
            scratch_shapes=scratch,
        ),
        out_shape=[jax.ShapeDtypeStruct(shape, kind) for shape, kind in outs],
        cost_estimate=estimate(micros),
    )(*meta, *operands)


def swap(values, distance, count):
    return lax.ppermute(values, "narrow", [(place, place ^ distance) for place in range(count)])


def gather_narrow(own, count):
    pieces = {0: own}
    distance = count // 2
    while distance:
        for place in sorted(pieces):
            pieces[place | distance] = swap(pieces[place], distance, count)
        distance //= 2
    return [pieces[place] for place in range(count)]


def reduce_narrow(keep, send, sums, count, width):
    slots = keep.shape[0]
    tailed = sums is not None
    received = swap(send, 1, count)
    terms = [(keep, 1), (received, 1)]
    blocks = count // 2
    distance = 2
    while distance < count:
        blocks //= 2
        operands = []
        specs = []
        for block in range(blocks):
            for term, stride in terms:
                operands.append(term)
                specs.append(striped(width, column=(2 * block + 1) * stride))
        lanes = blocks * width
        outs = [((slots + TAIL * tailed, lanes), bf16)]
        if tailed:
            operands += [received, sums]
            specs += [tail_spec(received.shape[1], slots), whole(sums.shape)]
            outs.append((sums.shape, f32))
        body = functools.partial(
            near_kernel, blocks=blocks, terms=len(terms), width=width, slots=slots, tailed=tailed
        )
        going, *rest = glue_call(
            body, (), operands, specs, outs, [whole(shape) for shape, _ in outs], slots // GLUE
        )
        if tailed:
            sums = rest[0]
        received = swap(going, distance, count)
        terms = [(term, 2 * stride) for term, stride in terms] + [(received, 1)]
        distance *= 2
    return [term for term, _ in terms], sums


def reduce_wide(parts, wide_count):
    bits = wide_count.bit_length() - 1
    index = lax.axis_index("wide")
    states = []
    for place, part in enumerate(parts):
        order = list(range(bits))
        if place % 2 and bits > 1:
            order[0], order[1] = order[1], order[0]
        states.append((part.reshape((2,) * bits + part.shape[1:]), order, list(range(bits))[::-1]))
    for stage in range(bits):
        moved = []
        for part, order, axes in states:
            bit = order[stage]
            axis = axes.index(bit)
            mine = (index >> bit) & 1
            going = lax.dynamic_index_in_dim(part, 1 - mine, axis, keepdims=False)
            received = lax.ppermute(
                going, "wide", [(at, at ^ (1 << bit)) for at in range(wide_count)]
            )
            moved.append((axis, mine, received))
        for place, (axis, mine, received) in enumerate(moved):
            part, order, axes = states[place]
            staying = lax.dynamic_index_in_dim(part, mine, axis, keepdims=False)
            total = staying.astype(f32) + received.astype(f32)
            if stage + 1 < bits:
                total = total.astype(bf16)
            del axes[axis]
            states[place] = (total, order, axes)
    return [part for part, _, _ in states]


def rotary_rows(slots):
    half = HEAD_DIM // 2
    inverse = theta_base ** (-2.0 * jnp.arange(half, dtype=f32) / HEAD_DIM)
    angles = jnp.arange(slots, dtype=f32)[:, None] * inverse[None, :]
    cos = jnp.cos(angles)
    sin = jnp.sin(angles)
    none = jnp.zeros_like(sin)
    copies = 128 // HEAD_DIM
    return (
        jnp.tile(jnp.concatenate([cos, cos], axis=1), (1, copies)),
        jnp.tile(jnp.concatenate([-sin, none], axis=1), (1, copies)),
        jnp.tile(jnp.concatenate([none, sin], axis=1), (1, copies)),
    )


def shards(
    inputs,
    lengths,
    attn_gain,
    attn_in_weight,
    attn_out_weight,
    mlp_gain,
    mlp_in_weight,
    mlp_out_weight,
    cotangent,
):
    count = lax.axis_size("narrow")
    wide_count = lax.axis_size("wide")
    index = lax.axis_index("narrow").astype(jnp.int32)
    tokens, width = inputs.shape
    full = width * count
    seq_count = lengths.shape[0]
    slots = tokens // seq_count
    heads = width // HEAD_DIM
    hidden = mlp_in_weight.shape[2]
    half = count // 2 * width
    tables = rotary_rows(slots)
    seqs = range(seq_count)
    blocks = slots // GLUE
    meta = (index.reshape(1), lengths)

    attn_weight = lax.all_gather(
        jnp.concatenate([attn_in_weight, attn_out_weight.T[None]]), "wide", axis=1, tiled=True
    )
    mlp_weight = lax.all_gather(
        jnp.concatenate([mlp_in_weight, mlp_out_weight.T[None]]), "wide", axis=1, tiled=True
    )
    input_pieces = gather_narrow(inputs, count)
    grad_pieces = gather_narrow(cotangent, count)
    attn_gain_rows = attn_gain.reshape(count, width)
    mlp_gain_rows = mlp_gain.reshape(count, width)

    def seq_spec(seq):
        return pl.BlockSpec((slots, width), lambda step, *scalars: (seq, 0))

    row_spec = whole((slots, width))
    table_specs = [whole((slots, 128))] * 3
    gain_spec = whole((count, width))
    attn_spec = whole(attn_weight.shape)
    sizes = dict(count=count, width=width, slots=slots, full=full)

    def forward_call(seq, earlier):
        return call_kernel(
            functools.partial(attend_kernel, seq=seq, heads=heads, **sizes),
            meta,
            [*input_pieces, attn_gain_rows, attn_weight, *tables],
            [seq_spec(seq)] * count + [gain_spec, attn_spec] + table_specs,
            [((slots, full), bf16)]
            + [((slots, width), bf16)] * 4
            + [((max(heads, STAT_ROWS), slots), f32), ((STAT_ROWS, slots), f32)]
            + [((slots, half), bf16), ((slots, half), bf16)],
            [pltpu.VMEM((width, slots), bf16), pltpu.VMEM((width, BLOCK), f32)],
            24,
            earlier,
        )

    def middle_call(seq, earlier):
        return call_kernel(
            functools.partial(mlp_kernel, seq=seq, **sizes),
            meta,
            [*residual_pieces[seq], *grad_pieces, mlp_gain_rows, mlp_weight],
            [striped(width, rows=BLOCK)] * count
            + [striped(width, seq, slots // BLOCK, rows=BLOCK)] * count
            + [gain_spec, whole(mlp_weight.shape)],
            [((slots, full), bf16), ((slots, full), bf16), ((slots, hidden), bf16)]
            + [((2, slots, hidden), bf16), ((STAT_ROWS, slots), f32)]
            + [((slots, half), bf16)] * 3
            + [((slots + TAIL, half), bf16)],
            [pltpu.VMEM((STAT_ROWS, slots), f32)],
            20,
            earlier,
            slots // BLOCK,
            [striped(full, rows=BLOCK)] * 2
            + [striped(hidden, rows=BLOCK)]
            + [pl.BlockSpec((2, BLOCK, hidden), lambda step, *scalars: (0, step, 0))]
            + [pl.BlockSpec((STAT_ROWS, BLOCK), lambda step, *scalars: (0, step))]
            + [striped(half, rows=BLOCK)] * 3
            + [whole((slots + TAIL, half))],
        )

    def backward_call(seq, earlier):
        normed, queries, keys, values, attended, log_sum = forward[seq][:6]
        return call_kernel(
            functools.partial(attend_back_kernel, seq=seq, heads=heads, **sizes),
            meta,
            [*attn_grad_pieces[seq], queries, keys, values, attended, log_sum, normed]
            + [attn_gain_rows, attn_weight, *tables],
            [row_spec] * (count + 4)
            + [whole(log_sum.shape), whole((slots, full)), gain_spec, attn_spec]
            + table_specs,
            [((slots, full), bf16), ((3, slots, width), bf16), ((STAT_ROWS, slots), f32)]
            + [((slots, half), bf16), ((slots + TAIL, half), bf16)],
            [
                pltpu.VMEM((slots, width), bf16),
                pltpu.VMEM((max(heads, STAT_ROWS), slots), f32),
                pltpu.VMEM((width, slots), bf16),
                pltpu.VMEM((slots, heads * BLOCK), bf16),
                pltpu.VMEM((slots, heads * BLOCK), bf16),
                pltpu.VMEM((width, BLOCK), f32),
                pltpu.VMEM((slots, width), f32),
                pltpu.VMEM((slots, width), f32),
            ],
            26,
            earlier,
        )

    def norm_back_call(seq, parts, source, base, gains, target=None):
        terms, sums, stats = parts
        masked = target is None
        target = target or []
        outs = [((slots, width), f32), ((slots, width), bf16)]
        out_specs = [striped(width)] * 2
        if not masked:
            outs = [((tokens, width), f32)]
            out_specs = [striped(width, seq, blocks)]
        return glue_call(
            functools.partial(
                norm_back_kernel, seq=seq, terms=len(terms), slots=slots, full=full, masked=masked
            ),
            meta,
            [*terms, terms[-1], sums, stats, source[0], base[0], gains, *target],
            [striped(width)] * len(terms)
            + [tail_spec(width, slots)]
            + [whole(sums.shape), whole(stats.shape), source[1], base[1], gain_spec]
            + [pl.BlockSpec(memory_space=pl.ANY)] * len(target),
            [*outs, ((STAT_ROWS, width), f32)],
            [*out_specs, whole((STAT_ROWS, width))],
            blocks,
            [(8 + len(terms), 0)] * len(target),
        )

    forward, residuals, residual_pieces = [], [], []
    earlier = [grad_pieces[count // 2]]
    for seq in seqs:
        forward.append(forward_call(seq, earlier))
        earlier = [forward[seq][6]]
    for seq in seqs:
        terms, _ = reduce_narrow(forward[seq][7], forward[seq][8], None, count, width)
        residual, low = glue_call(
            residual_kernel,
            (),
            [inputs, *terms],
            [striped(width, seq, blocks)] + [striped(width)] * len(terms),
            [((slots, width), f32), ((slots, width), bf16)],
            [striped(width)] * 2,
            blocks,
        )
        residuals.append(residual)
        residual_pieces.append(gather_narrow(low, count))

    middle, grad_residuals, attn_grad_pieces = [], [], []
    mlp_gain_local = 0.0
    for seq in seqs:
        middle.append(middle_call(seq, earlier))
        earlier = [middle[seq][4]]
    for seq in seqs:
        terms, sums = reduce_narrow(middle[seq][7], middle[seq][8], middle[seq][4], count, width)
        grad_residual, low, gain_part = norm_back_call(
            seq,
            (terms, sums, middle[seq][4]),
            (residuals[seq], striped(width)),
            (cotangent, striped(width, seq, blocks)),
            mlp_gain_rows,
        )
        grad_residuals.append(grad_residual)
        mlp_gain_local = mlp_gain_local + gain_part[0]
        attn_grad_pieces.append(gather_narrow(low, count))
    mlp_grads = weight_grads(
        [
            ([middle[seq][0] for seq in seqs], [middle[seq][3] for seq in seqs]),
            ([middle[seq][1] for seq in seqs], [middle[seq][2][None] for seq in seqs]),
        ],
        wide_count,
        full,
        17,
        earlier,
    )
    mlp_shard = lax.psum_scatter(
        mlp_grads.reshape(-1, hidden), "wide", scatter_dimension=0, tiled=True
    )

    backward, output, inputs_grad = [], [], []
    earlier = [mlp_grads]
    for seq in seqs:
        backward.append(backward_call(seq, earlier))
        earlier = [backward[seq][2]]
    for seq in seqs:
        terms, _ = reduce_narrow(middle[seq][5], middle[seq][6], None, count, width)
        output = glue_call(
            functools.partial(output_kernel, seq=seq, terms=len(terms)),
            meta,
            [residuals[seq], *terms, *output],
            [striped(width)] * (1 + len(terms)) + [pl.BlockSpec(memory_space=pl.ANY)] * len(output),
            [((tokens, width), f32)],
            [striped(width, seq, blocks)],
            blocks,
            [(3 + len(terms), 0)] * len(output),
        )
    attn_grads = weight_grads(
        [
            ([forward[seq][0] for seq in seqs], [backward[seq][1] for seq in seqs]),
            ([backward[seq][0] for seq in seqs], [forward[seq][4][None] for seq in seqs]),
        ],
        wide_count,
        full,
        10,
        earlier,
    )
    mlp_shard = mlp_shard.reshape(mlp_grads.shape[1:])
    kinds, rows = attn_grads.shape[1:3]
    attn_shard = jnp.concatenate(
        reduce_wide(
            [
                attn_grads[:, start : start + kinds // 2].reshape(wide_count, -1, width)
                for start in range(0, kinds, kinds // 2)
            ],
            wide_count,
        )
    ).reshape(kinds, rows, width)

    attn_gain_local = 0.0
    for seq in seqs:
        terms, sums = reduce_narrow(
            backward[seq][3], backward[seq][4], backward[seq][2], count, width
        )
        *inputs_grad, gain_part = norm_back_call(
            seq,
            (terms, sums, forward[seq][6]),
            (inputs, striped(width, seq, blocks)),
            (grad_residuals[seq], striped(width)),
            attn_gain_rows,
            inputs_grad,
        )
        attn_gain_local = attn_gain_local + gain_part[0]
    gain_grads = jnp.sum(
        lax.all_gather(jnp.stack([attn_gain_local, mlp_gain_local]), "wide"), axis=0
    )
    return (
        output[0],
        inputs_grad[0],
        gain_grads[0],
        attn_shard[:3],
        attn_shard[3].T,
        gain_grads[1],
        mlp_shard[:2].astype(f32),
        mlp_shard[2].T.astype(f32),
    )


def solution(mesh):
    in_specs = (
        P("wide", "narrow"),
        P("wide"),
        P(),
        P(None, "wide", "narrow"),
        P("narrow", "wide"),
        P(),
        P(None, "wide", "narrow"),
        P("narrow", "wide"),
        P("wide", "narrow"),
    )
    out_specs = (
        P("wide", "narrow"),
        P("wide", "narrow"),
        P("narrow"),
        P(None, "wide", "narrow"),
        P("narrow", "wide"),
        P("narrow"),
        P(None, "wide", "narrow"),
        P("narrow", "wide"),
    )
    return jax.shard_map(shards, mesh=mesh, in_specs=in_specs, out_specs=out_specs, check_vma=False)
```

profile of v0, /device:TPU:0, one launch (start us, length us, event | category | flops | bytes accessed | tf_op | source)
XLA Modules:
  0.0 460.3 jit_solution(14717029872883713866)
XLA Ops:
  13.1 24.1 %collective-permute-done.1.refs_4_ = bf16[2048,256]{1,0:T(8,128)(2,1)S(1)} collective-permute-done((bf16[2048,256]{1,0:T(8,128)(2,1)}, bf16[2048,256]{1,0:T(8,128)(2,1)S(1)}, u32[]{:S(2)}, u32[]{:S(2)}) %collective-permute-start.1) | collective-permute-done | bytes 1048608 | tf_op jit(solution)/shard_map/ppermute | solution.py:523
  44.9 13.9 %collective-permute-done.3.refs_11_.refs_8_ = bf16[2048,256]{1,0:T(8,128)(2,1)S(1)} collective-permute-done((bf16[2048,256]{1,0:T(8,128)(2,1)}, bf16[2048,256]{1,0:T(8,128)(2,1)S(1)}, u32[]{:S(2)}, u32[]{:S(2)}) %collective-permute-start.3) | collective-permute-done | bytes 1048608 | tf_op jit(solution)/shard_map/ppermute | solution.py:523
  62.6 23.9 %shard_map.152 = (bf16[1024,1024]{1,0:T(8,128)(2,1)}, bf16[1024,256]{1,0:T(8,128)(2,1)}, bf16[1024,256]{1,0:T(8,128)(2,1)}, bf16[1024,256]{1,0:T(8,128)(2,1)}, b...) custom-call(s32[1]{0:T(128)} %bitcast.1.refs_0_.place_ref, ...), custom_call_target="tpu_custom_call" | custom-call | flops 24000000000 | bytes 1048576 | tf_op jit(solution)/shard_map/pallas_call | solution.py:508
  86.4 24.2 %shard_map.153 = (bf16[1024,1024]{1,0:T(8,128)(2,1)}, bf16[1024,256]{1,0:T(8,128)(2,1)}, bf16[1024,256]{1,0:T(8,128)(2,1)}, bf16[1024,256]{1,0:T(8,128)(2,1)}, b...) custom-call(s32[1]{0:T(128)} %bitcast.1.refs_0_.place_ref, ...), custom_call_target="tpu_custom_call" | custom-call | flops 24000000000 | bytes 1048576 | tf_op jit(solution)/shard_map/pallas_call | solution.py:508
  120.0 9.4 %collective-permute-done.12.refs_2_ = bf16[1024,256]{1,0:T(8,128)(2,1)} collective-permute-done((bf16[1024,256]{1,0:T(8,128)(2,1)}, bf16[1024,256]{1,0:T(8,128)(2,1)}, u32[]{:S(2)}, u32[]{:S(2)}) %collective-permute-start.12) | collective-permute-done | bytes 524320 | tf_op jit(solution)/shard_map/ppermute | solution.py:523
  133.3 7.2 %collective-permute-done.5.refs_2_ = bf16[1024,256]{1,0:T(8,128)(2,1)} collective-permute-done((bf16[1024,256]{1,0:T(8,128)(2,1)}, bf16[1024,256]{1,0:T(8,128)(2,1)}, u32[]{:S(2)}, u32[]{:S(2)}) %collective-permute-start.5) | collective-permute-done | bytes 524320 | tf_op jit(solution)/shard_map/ppermute | solution.py:523
  144.5 7.3 %collective-permute-done.14.refs_4_ = bf16[1024,256]{1,0:T(8,128)(2,1)} collective-permute-done((bf16[1024,256]{1,0:T(8,128)(2,1)}, bf16[1024,256]{1,0:T(8,128)(2,1)}, u32[]{:S(2)}, u32[]{:S(2)}) %collective-permute-start.14) | collective-permute-done | bytes 524320 | tf_op jit(solution)/shard_map/ppermute | solution.py:523
  152.9 9.2 %collective-permute-done.7.refs_4_ = bf16[1024,256]{1,0:T(8,128)(2,1)} collective-permute-done((bf16[1024,256]{1,0:T(8,128)(2,1)}, bf16[1024,256]{1,0:T(8,128)(2,1)}, u32[]{:S(2)}, u32[]{:S(2)}) %collective-permute-start.7) | collective-permute-done | bytes 524320 | tf_op jit(solution)/shard_map/ppermute | solution.py:523
  162.1 20.4 %shard_map.158 = (bf16[1024,1024]{1,0:T(8,128)(2,1)}, bf16[1024,1024]{1,0:T(8,128)(2,1)}, bf16[1024,656]{1,0:T(8,128)(2,1)}, bf16[2,1024,656]{2,1,0:T(8,128)(2,1...) custom-call(s32[1]{0:T(128)} %bitcast.1.refs_0_.place_ref, ...), custom_call_target="tpu_custom_call" | custom-call | flops 20000000000 | bytes 1048576 | tf_op jit(solution)/shard_map/pallas_call | solution.py:508
  184.0 20.4 %shard_map.159 = (bf16[1024,1024]{1,0:T(8,128)(2,1)}, bf16[1024,1024]{1,0:T(8,128)(2,1)}, bf16[1024,656]{1,0:T(8,128)(2,1)}, bf16[2,1024,656]{2,1,0:T(8,128)(2,1...) custom-call(s32[1]{0:T(128)} %bitcast.1.refs_0_.place_ref, ...), custom_call_target="tpu_custom_call" | custom-call | flops 20000000000 | bytes 1048576 | tf_op jit(solution)/shard_map/pallas_call | solution.py:508
  213.1 10.1 %collective-permute-done.26.refs_2_.refs_3_ = bf16[1040,256]{1,0:T(8,128)(2,1)S(1)} collective-permute-done((bf16[1040,256]{1,0:T(8,128)(2,1)}, bf16[1040,256]{1,0:T(8,128)(2,1)S(1)}, u32[]{:S(2)}, u32[]{:S(2)}) %collective-permute-start.26) | collective-permute-done | bytes 532512 | tf_op jit(solution)/shard_map/ppermute | solution.py:523
  224.0 4.6 %shard_map.167 = (f32[1024,256]{1,0:T(8,128)}, bf16[1024,256]{1,0:T(8,128)(2,1)}, f32[8,256]{1,0:T(8,128)}) custom-call(s32[1]{0:T(128)} %bitcast.1.refs_0_.place_ref, s32[2]{0:T(128)} %lengths.11, bf16[1024,512]{1,0:T(8,128)(2,1)} %get-tuple-element.103.refs_0_, bf16[1040,512]{1,0:T(8,128)(2,1)} %copy-done.7, bf16[1040,256]{1,0:T(8,128)(2,1)} %copy-done.18, ...), custom_call_target="tpu_custom_call" | custom-call | flops 2000000000 | bytes 1048576 | tf_op jit(solution)/shard_map/pallas_call | solution.py:493
  235.4 4.5 shard_map.165
  241.4 4.6 collective-permute-done.28.refs_4_
  246.0 25.1 %shard_map.168.refs_17_ = bf16[8,3,128,656]{3,2,1,0:T(8,128)(2,1)} custom-call(bf16[1024,1024]{1,0:T(8,128)(2,1)} %get-tuple-element.114.refs_0_, bf16[1024,1024]{1,0:T(8,128)(2,1)} %get-tuple-element.115.refs_1_, bf16[2,1024,656]{2,1,0:T(8,128)(2,1)} %get-tuple-element.116.refs_2_, bf16[2,1024,656]{2,1,0:T(8,128)(2,1)} %get-tuple-element.117.refs_3_, ...), custom_call_target="tpu_custom_call" | custom-call | flops 16999999488 | bytes 1048576 | tf_op jit(solution)/shard_map/pallas_call | solution.py:456
  279.5 26.1 %shard_map.169 = (bf16[1024,1024]{1,0:T(8,128)(2,1)}, bf16[3,1024,256]{2,1,0:T(8,128)(2,1)}, f32[8,1024]{1,0:T(8,128)}, bf16[1024,512]{1,0:T(8,128)(2,1)}, bf16[1040,512]{1,0:T(8,128)(2,1)}) custom-call(s32[1]{0:T(128)} %bitcast.1.refs_0_.place_ref, s32[2]{0:T(128)} %lengths.11, bf16[1024,256]{1,0:T(8,128)(2,1)} %get-tuple-element.107.refs_2_, ...), custom_call_target="tpu_custom_call" | custom-call | flops 25999998976 | bytes 1048576 | tf_op jit(solution)/shard_map/pallas_call | solution.py:508
  306.5 26.3 %shard_map.170 = (bf16[1024,1024]{1,0:T(8,128)(2,1)}, bf16[3,1024,256]{2,1,0:T(8,128)(2,1)}, f32[8,1024]{1,0:T(8,128)}, bf16[1024,512]{1,0:T(8,128)(2,1)}, bf16[1040,512]{1,0:T(8,128)(2,1)}) custom-call(s32[1]{0:T(128)} %bitcast.1.refs_0_.place_ref, s32[2]{0:T(128)} %lengths.11, bf16[1024,256]{1,0:T(8,128)(2,1)} %get-tuple-element.96.refs_2_, ...), custom_call_target="tpu_custom_call" | custom-call | flops 25999998976 | bytes 1048576 | tf_op jit(solution)/shard_map/pallas_call | solution.py:508
  332.8 9.6 %shard_map.175 = bf16[8,4,128,256]{3,2,1,0:T(8,128)(2,1)} custom-call(bf16[1024,1024]{1,0:T(8,128)(2,1)} %get-tuple-element.113.refs_11_.refs_0_, bf16[1024,1024]{1,0:T(8,128)(2,1)} %get-tuple-element.102.refs_11_.refs_1_, bf16[3,1024,256]{2,1,0:T(8,128)(2,1)} %get-tuple-element.140.refs_2_, bf16[3,1024,256]{2,1,0:T(8,128)(2,1)} %get-tuple-element.141.refs_3_, ...), custom_call_target="tpu_custom_call" | custom-call | flops 10000000000 | bytes 1048576 | tf_op jit(solution)/shard_map/pallas_call | solution.py:456
  352.1 6.3 %collective-permute-done.37 = bf16[2,2,256,256]{3,2,0,1:T(8,128)(2,1)S(1)} collective-permute-done((bf16[2,2,256,256]{3,2,0,1:T(8,128)(2,1)S(1)}, bf16[2,2,256,256]{3,2,0,1:T(8,128)(2,1)S(1)}, u32[]{:S(2)}, u32[]{:S(2)}) %collective-permute-start.37) | collective-permute-done | bytes 524320 | tf_op jit(solution)/shard_map/ppermute | solution.py:587
  359.1 7.8 %collective-permute-done.34 = bf16[2,2,256,256]{3,2,0,1:T(8,128)(2,1)S(1)} collective-permute-done((bf16[2,2,256,256]{3,2,0,1:T(8,128)(2,1)S(1)}, bf16[2,2,256,256]{3,2,0,1:T(8,128)(2,1)S(1)}, u32[]{:S(2)}, u32[]{:S(2)}) %collective-permute-start.34) | collective-permute-done | bytes 524320 | tf_op jit(solution)/shard_map/ppermute | solution.py:587
  367.8 7.0 %collective-permute-done.38 = bf16[2,256,256]{2,1,0:T(8,128)(2,1)S(1)} collective-permute-done((bf16[2,256,256]{2,1,0:T(8,128)(2,1)S(1)}, bf16[2,256,256]{2,1,0:T(8,128)(2,1)S(1)}, u32[]{:S(2)}, u32[]{:S(2)}) %collective-permute-start.38) | collective-permute-done | bytes 262176 | tf_op jit(solution)/shard_map/ppermute | solution.py:587
  374.9 15.4 %collective-permute-done.35 = bf16[2,256,256]{2,1,0:T(8,128)(2,1)S(1)} collective-permute-done((bf16[2,256,256]{2,1,0:T(8,128)(2,1)S(1)}, bf16[2,256,256]{2,1,0:T(8,128)(2,1)S(1)}, u32[]{:S(2)}, u32[]{:S(2)}) %collective-permute-start.35) | collective-permute-done | bytes 262176 | tf_op jit(solution)/shard_map/ppermute | solution.py:587
  399.3 9.3 %collective-permute-done.33.refs_2_.refs_3_ = bf16[1040,256]{1,0:T(8,128)(2,1)S(1)} collective-permute-done((bf16[1040,256]{1,0:T(8,128)(2,1)}, bf16[1040,256]{1,0:T(8,128)(2,1)S(1)}, u32[]{:S(2)}, u32[]{:S(2)}) %collective-permute-start.33) | collective-permute-done | bytes 532512 | tf_op jit(solution)/shard_map/ppermute | solution.py:523
  422.7 26.1 %all-gather.1 = f32[8,2,256]{2,1,0:T(2,128)S(1)} all-gather(f32[1,2,256]{2,1,0:T(2,128)S(1)} %maximum_bitcast_fusion), channel_id=2, replica_groups=mesh['wide'=8,'narrow'=4] {'wide'}, dimensions={0}, use_global_device_ids=true | all-gather | bytes 18432 | tf_op jit(solution)/shard_map/all_gather | solution.py:857
  (187 shorter events, 103.4 us)
Async XLA Ops:
  7.2 55.4 %all-gather.5.cloned.1.call-start = ((), (), s32[]{:S(2)}) async-start(), calls=%async_computation.1 | async-start | bytes 2359296 | tf_op jit(solution)/shard_map/all_gather | solution.py:643
  9.8 152.3 %all-gather.7.cloned.1.call-start = ((), (), s32[]{:S(2)}) async-start(), calls=%async_computation.2 | async-start | bytes 5308416 | tf_op jit(solution)/shard_map/all_gather | solution.py:646
  9.9 27.3 %collective-permute-start.1 = (bf16[2048,256]{1,0:T(8,128)(2,1)}, bf16[2048,256]{1,0:T(8,128)(2,1)S(1)}, u32[]{:S(2)}, u32[]{:S(2)}) collective-permute-start(bf16[2048,256]{1,0:T(8,128)(2,1)} %refs_6_.7), channel_id=1, source_target_pairs={{0,2},{1,3},{2,0},{3,1},{4,6},{5,7},{6,4},{7,5},{8,10},{9,11},{10,... | collective-permute-start | bytes 3145736 | tf_op jit(solution)/shard_map/ppermute | solution.py:523
  12.9 45.8 %collective-permute-start = (bf16[2048,256]{1,0:T(8,128)(2,1)}, bf16[2048,256]{1,0:T(8,128)(2,1)}, u32[]{:S(2)}, u32[]{:S(2)}) collective-permute-start(bf16[2048,256]{1,0:T(8,128)(2,1)} %refs_6_.7), channel_id=1, source_target_pairs={{0,1},{1,0},{2,3},{3,2},{4,5},{5,4},{6,7},{7,6},{8,9},{9,8},{10,11... | collective-permute-start | bytes 3145736 | tf_op jit(solution)/shard_map/ppermute | solution.py:523
  12.9 45.8 %collective-permute-start.3 = (bf16[2048,256]{1,0:T(8,128)(2,1)}, bf16[2048,256]{1,0:T(8,128)(2,1)S(1)}, u32[]{:S(2)}, u32[]{:S(2)}) collective-permute-start(bf16[2048,256]{1,0:T(8,128)(2,1)} %refs_7_.3), channel_id=1, source_target_pairs={{0,2},{1,3},{2,0},{3,1},{4,6},{5,7},{6,4},{7,5},{8,10},{9,11},{10,... | collective-permute-start | bytes 3145736 | tf_op jit(solution)/shard_map/ppermute | solution.py:523
  40.4 408.9 %reduce-scatter.4.cloned.1.call-start = ((), (), s32[]{:S(2)}) async-start(), calls=%async_computation.3 | async-start | bytes 5308416
  86.4 24.7 %collective-permute-start.11 = (bf16[1024,512]{1,0:T(8,128)(2,1)}, bf16[1024,512]{1,0:T(8,128)(2,1)S(1)}, u32[]{:S(2)}, u32[]{:S(2)}) collective-permute-start(bf16[1024,512]{1,0:T(8,128)(2,1)} %get-tuple-element.82), channel_id=1, source_target_pairs={{0,1},{1,0},{2,3},{3,2},{4,5},{5,4},{6,7},{7,6},{8,9},{9,8},{10,11... | collective-permute-start | bytes 3145736 | tf_op jit(solution)/shard_map/ppermute | solution.py:523
  119.4 33.0 %collective-permute-start.9 = (bf16[2048,256]{1,0:T(8,128)(2,1)S(1)}, bf16[2048,256]{1,0:T(8,128)(2,1)S(1)}, u32[]{:S(2)}, u32[]{:S(2)}) collective-permute-start(bf16[2048,256]{1,0:T(8,128)(2,1)S(1)} %copy-done.8), channel_id=1, source_target_pairs={{0,1},{1,0},{2,3},{3,2},{4,5},{5,4},{6,7},{7,6},{8,9},{9,8},{10,11... | collective-permute-start | bytes 3145736 | tf_op jit(solution)/shard_map/ppermute | solution.py:523
  119.5 42.6 %collective-permute-start.10 = (bf16[2048,256]{1,0:T(8,128)(2,1)S(1)}, bf16[2048,256]{1,0:T(8,128)(2,1)}, u32[]{:S(2)}, u32[]{:S(2)}) collective-permute-start(bf16[2048,256]{1,0:T(8,128)(2,1)S(1)} %copy-done.10), channel_id=1, source_target_pairs={{0,1},{1,0},{2,3},{3,2},{4,5},{5,4},{6,7},{7,6},{8,9},{9,8},{10,11... | collective-permute-start | bytes 3145736 | tf_op jit(solution)/shard_map/ppermute | solution.py:523
  152.4 30.6 %collective-permute-start.6 = (bf16[1024,256]{1,0:T(8,128)(2,1)}, bf16[1024,256]{1,0:T(8,128)(2,1)S(1)}, u32[]{:S(2)}, u32[]{:S(2)}) collective-permute-start(bf16[1024,256]{1,0:T(8,128)(2,1)} %get-tuple-element.80.refs_2_), channel_id=1, source_target_pairs={{0,1},{1,0},{2,3},{3,2},{4,5},{5,4},{6,7},{7,6},{8,9},{9,8},{10,11... | collective-permute-start | bytes 1572872 | tf_op jit(solution)/shard_map/ppermute | solution.py:523
  182.5 22.5 %collective-permute-start.25 = (bf16[1040,512]{1,0:T(8,128)(2,1)}, bf16[1040,512]{1,0:T(8,128)(2,1)S(1)}, u32[]{:S(2)}, u32[]{:S(2)}) collective-permute-start(bf16[1040,512]{1,0:T(8,128)(2,1)} %get-tuple-element.104), channel_id=1, source_target_pairs={{0,1},{1,0},{2,3},{3,2},{4,5},{5,4},{6,7},{7,6},{8,9},{9,8},{10,11... | collective-permute-start | bytes 3194888 | tf_op jit(solution)/shard_map/ppermute | solution.py:523
  204.5 25.7 %collective-permute-start.18 = (bf16[1024,512]{1,0:T(8,128)(2,1)}, bf16[1024,512]{1,0:T(8,128)(2,1)}, u32[]{:S(2)}, u32[]{:S(2)}) collective-permute-start(bf16[1024,512]{1,0:T(8,128)(2,1)} %get-tuple-element.90), channel_id=1, source_target_pairs={{0,1},{1,0},{2,3},{3,2},{4,5},{5,4},{6,7},{7,6},{8,9},{9,8},{10,11... | collective-permute-start | bytes 3145736 | tf_op jit(solution)/shard_map/ppermute | solution.py:523
  212.6 22.1 %collective-permute-start.21 = (bf16[1040,256]{1,0:T(8,128)(2,1)}, bf16[1040,256]{1,0:T(8,128)(2,1)S(1)}, u32[]{:S(2)}, u32[]{:S(2)}) collective-permute-start(bf16[1040,256]{1,0:T(8,128)(2,1)} %get-tuple-element.94), channel_id=1, source_target_pairs={{0,2},{1,3},{2,0},{3,1},{4,6},{5,7},{6,4},{7,5},{8,10},{9,11},{10,... | collective-permute-start | bytes 1597448 | tf_op jit(solution)/shard_map/ppermute | solution.py:523
  230.2 40.9 %collective-permute-start.16 = (bf16[1024,512]{1,0:T(8,128)(2,1)S(1)}, bf16[1024,512]{1,0:T(8,128)(2,1)S(1)}, u32[]{:S(2)}, u32[]{:S(2)}) collective-permute-start(bf16[1024,512]{1,0:T(8,128)(2,1)S(1)} %copy-done.11), channel_id=1, source_target_pairs={{0,1},{1,0},{2,3},{3,2},{4,5},{5,4},{6,7},{7,6},{8,9},{9,8},{10,11... | collective-permute-start | bytes 3145736 | tf_op jit(solution)/shard_map/ppermute | solution.py:523
  232.3 43.3 %collective-permute-start.19 = (bf16[1024,256]{1,0:T(8,128)(2,1)}, bf16[1024,256]{1,0:T(8,128)(2,1)}, u32[]{:S(2)}, u32[]{:S(2)}) collective-permute-start(bf16[1024,256]{1,0:T(8,128)(2,1)} %shard_map.161), channel_id=1, source_target_pairs={{0,2},{1,3},{2,0},{3,1},{4,6},{5,7},{6,4},{7,5},{8,10},{9,11},{10,... | collective-permute-start | bytes 1572872 | tf_op jit(solution)/shard_map/ppermute | solution.py:523
  232.9 46.6 %collective-permute-start.27 = (bf16[1024,256]{1,0:T(8,128)(2,1)S(1)}, bf16[1024,256]{1,0:T(8,128)(2,1)}, u32[]{:S(2)}, u32[]{:S(2)}) collective-permute-start(bf16[1024,256]{1,0:T(8,128)(2,1)S(1)} %copy-done.19), channel_id=1, source_target_pairs={{0,1},{1,0},{2,3},{3,2},{4,5},{5,4},{6,7},{7,6},{8,9},{9,8},{10,11... | collective-permute-start | bytes 1572872 | tf_op jit(solution)/shard_map/ppermute | solution.py:523
  239.9 39.2 %collective-permute-start.23 = (bf16[1024,256]{1,0:T(8,128)(2,1)}, bf16[1024,256]{1,0:T(8,128)(2,1)}, u32[]{:S(2)}, u32[]{:S(2)}) collective-permute-start(bf16[1024,256]{1,0:T(8,128)(2,1)} %get-tuple-element.96.refs_2_), channel_id=1, source_target_pairs={{0,2},{1,3},{2,0},{3,1},{4,6},{5,7},{6,4},{7,5},{8,10},{9,11},{10,... | collective-permute-start | bytes 1572872 | tf_op jit(solution)/shard_map/ppermute | solution.py:523
  246.0 33.5 %collective-permute-start.29 = (bf16[1024,256]{1,0:T(8,128)(2,1)}, bf16[1024,256]{1,0:T(8,128)(2,1)}, u32[]{:S(2)}, u32[]{:S(2)}) collective-permute-start(bf16[1024,256]{1,0:T(8,128)(2,1)} %collective-permute-done.28.refs_4_), channel_id=1, source_target_pairs={{0,1},{1,0},{2,3},{3,2},{4,5},{5,4},{6,7},{7,6},{8,9},{9,8},{10,11... | collective-permute-start | bytes 1572872 | tf_op jit(solution)/shard_map/ppermute | solution.py:523
  274.1 70.2 %collective-permute-start.17 = (bf16[1024,256]{1,0:T(8,128)(2,1)}, bf16[1024,256]{1,0:T(8,128)(2,1)S(1)}, u32[]{:S(2)}, u32[]{:S(2)}) collective-permute-start(bf16[1024,256]{1,0:T(8,128)(2,1)} %shard_map.160), channel_id=1, source_target_pairs={{0,2},{1,3},{2,0},{3,1},{4,6},{5,7},{6,4},{7,5},{8,10},{9,11},{10,... | collective-permute-start | bytes 1572872 | tf_op jit(solution)/shard_map/ppermute | solution.py:523
  278.9 26.6 %collective-permute-start.22 = (bf16[1024,256]{1,0:T(8,128)(2,1)S(1)}, bf16[1024,256]{1,0:T(8,128)(2,1)S(1)}, u32[]{:S(2)}, u32[]{:S(2)}) collective-permute-start(bf16[1024,256]{1,0:T(8,128)(2,1)S(1)} %copy-done.20), channel_id=1, source_target_pairs={{0,1},{1,0},{2,3},{3,2},{4,5},{5,4},{6,7},{7,6},{8,9},{9,8},{10,11... | collective-permute-start | bytes 1572872 | tf_op jit(solution)/shard_map/ppermute | solution.py:523
  279.1 26.5 %collective-permute-start.24 = (bf16[1024,256]{1,0:T(8,128)(2,1)}, bf16[1024,256]{1,0:T(8,128)(2,1)S(1)}, u32[]{:S(2)}, u32[]{:S(2)}) collective-permute-start(bf16[1024,256]{1,0:T(8,128)(2,1)} %collective-permute-done.23.refs_4_), channel_id=1, source_target_pairs={{0,1},{1,0},{2,3},{3,2},{4,5},{5,4},{6,7},{7,6},{8,9},{9,8},{10,11... | collective-permute-start | bytes 1572872 | tf_op jit(solution)/shard_map/ppermute | solution.py:523
  351.6 39.8 %collective-permute-start.32 = (bf16[1040,512]{1,0:T(8,128)(2,1)}, bf16[1040,512]{1,0:T(8,128)(2,1)}, u32[]{:S(2)}, u32[]{:S(2)}) collective-permute-start(bf16[1040,512]{1,0:T(8,128)(2,1)} %get-tuple-element.130), channel_id=1, source_target_pairs={{0,1},{1,0},{2,3},{3,2},{4,5},{5,4},{6,7},{7,6},{8,9},{9,8},{10,11... | collective-permute-start | bytes 3194888 | tf_op jit(solution)/shard_map/ppermute | solution.py:523
  351.6 43.2 %collective-permute-start.30 = (bf16[1040,512]{1,0:T(8,128)(2,1)}, bf16[1040,512]{1,0:T(8,128)(2,1)S(1)}, u32[]{:S(2)}, u32[]{:S(2)}) collective-permute-start(bf16[1040,512]{1,0:T(8,128)(2,1)} %get-tuple-element.124), channel_id=1, source_target_pairs={{0,1},{1,0},{2,3},{3,2},{4,5},{5,4},{6,7},{7,6},{8,9},{9,8},{10,11... | collective-permute-start | bytes 3194888 | tf_op jit(solution)/shard_map/ppermute | solution.py:523
  367.0 23.3 %collective-permute-start.35 = (bf16[2,256,256]{2,1,0:T(8,128)(2,1)S(1)}, bf16[2,256,256]{2,1,0:T(8,128)(2,1)S(1)}, u32[]{:S(2)}, u32[]{:S(2)}) collective-permute-start(bf16[2,256,256]{2,1,0:T(8,128)(2,1)S(1)} %dynamic-slice_bitcast_fusion.1), channel_id=1, source_target_pairs={{0,8},{4,12},{8,0},{12,4},{16,24},{20,28},{24,16},{28,20},{1,9},{5... | collective-permute-start | bytes 786440 | tf_op jit(solution)/shard_map/ppermute | solution.py:587
  (44 other events, 399.5 us)
Sparse Core Ops, SparseCore 0:
  10.7 51.7 all-gather.4
  65.3 77.8 all-gather.6
  271.2 120.3 reduce-scatter.3
where the time goes:
time: 470 us; the launch traced here: 460 us
  Pallas kernels  222 us (47%)
  waiting for transfers between devices  140 us (30%)
  blocking collectives  26.1 us (6%)
  local copies, waits for them, and re-layouts  25.1 us (5%)
  starting transfers between devices  25.1 us (5%)
  between operations  14.6 us (3%)
  other arithmetic  7.44 us (2%)
    pallas_call x6, Pallas kernels, call_kernel(): pl.pallas_call(body, grid_spec=pltpu.PrefetchScalarGridSpec(num_scalar_pr...  141 us
    ppermute x34, waiting for transfers between devices, swap(): lax.ppermute(values, 'narrow', [(place, place ^ distance) for place in ra...  99.6 us
    pallas_call x16, Pallas kernels, glue_call(): pl.pallas_call(body, grid_spec=pltpu.PrefetchScalarGridSpec(num_scalar_pr...  46.2 us
    ppermute x6, waiting for transfers between devices, reduce_wide(): lax.ppermute(going, 'wide', [(at, at ^ 1 << bit) for at in range(wide_cou...  36.4 us
    pallas_call x2, Pallas kernels, weight_grads(): pl.pallas_call(body, grid=(wide_count // per_step,), in_specs=specs, out_...  34.6 us
    all_gather x1, blocking collectives, shards(): lax.all_gather(jnp.stack([attn_gain_local, mlp_gain_local]), 'wide')  26.1 us
    ppermute x34, starting transfers between devices, swap(): lax.ppermute(values, 'narrow', [(place, place ^ distance) for place in ra...  21.1 us
    unnamed x56, local copies, waits for them, and re-layouts  16.2 us
  transfers between devices with their start and end apart: 43, of which 16 were waited for; matrix products, arithmetic and copies ran while one was open for 3% of the time, Pallas kernels for 48%

commit v1 on v0

--- a/solution.py
+++ b/solution.py
@@ -40,6 +40,16 @@
     return pl.ds(pl.multiple_of((index ^ distance) * width, width), width)
 
 
+def stacked(ref, start, rows, chunks=None):
+    part = ref[slice(None) if chunks is None else chunks, start : start + rows, :]
+    return part.reshape(part.shape[0] * rows, part.shape[2])
+
+
+def chunk_block(index, distance, width, rows):
+    per_block = width // rows
+    return pl.ds((index ^ distance) * per_block, per_block)
+
+
 def norm_parts(parts, full):
     mean = sum(jnp.sum(part, axis=-1, keepdims=True) for part in parts) / full
     parts = [part - mean for part in parts]
@@ -73,6 +83,15 @@
     return jnp.where(inside, values.astype(f32), 0.0).astype(bf16)
 
 
+def head_pairs(heads, one_head):
+    def pair(place, carry):
+        one_head(2 * place)
+        one_head(2 * place + 1)
+        return carry
+
+    lax.fori_loop(0, heads // 2, pair, 0)
+
+
 def send_tail(send, slots, first, second):
     lanes = send.shape[1]
     pieces = [row[:, start : start + lanes] for row in (first, second) for start in range(0, slots, lanes)]
@@ -83,9 +102,10 @@
 
 def attend_kernel(place_ref, lengths, *refs, seq, count, width, heads, slots, full):
     pieces = refs[:count]
-    gain, weight, cos_ref, low_ref, high_ref = refs[count : count + 5]
-    normed, q_out, k_out, v_out, attended, log_sum, stats, keep, send = refs[count + 5 : count + 14]
-    values_t, out_t = refs[count + 14 :]
+    gain, first_weight, second_weight, cos_ref, low_ref, high_ref = refs[count : count + 6]
+    normed, q_out, k_out, v_out, attended, log_sum, stats, keep, send = refs[count + 6 : count + 15]
+    values_t, out_t = refs[count + 15 :]
+    chunk = first_weight.shape[1] // 2
     index = place_ref[0]
     length = lengths[seq]
     live = pl.cdiv(length, BLOCK)
@@ -99,11 +119,11 @@
             normed[rows, feature_block(index, place, width)] = gained.astype(bf16)
         stats[:, rows] = columns_to_rows((mean, factor))
         row = normed[rows, :]
-        turned = turn(dot_nn(row, weight[0]), cos_ref, low_ref, high_ref, rows, 1.0)
+        turned = turn(dot_nn(row, stacked(first_weight, 0, chunk)), cos_ref, low_ref, high_ref, rows, 1.0)
         q_out[rows, :] = (turned.astype(bf16).astype(f32) * HEAD_DIM**-0.5).astype(bf16)
-        turned = turn(dot_nn(row, weight[1]), cos_ref, low_ref, high_ref, rows, 1.0)
+        turned = turn(dot_nn(row, stacked(first_weight, chunk, chunk)), cos_ref, low_ref, high_ref, rows, 1.0)
         k_out[rows, :] = turned.astype(bf16)
-        v_out[rows, :] = dot_nn(row, weight[2]).astype(bf16)
+        v_out[rows, :] = dot_nn(row, stacked(second_weight, 0, chunk)).astype(bf16)
         return carry
 
     def clear(block, carry):
@@ -127,8 +147,9 @@
         def query_block(block, carry):
             rows = block_rows(block)
             queries = q_out[rows, :]
-            for head in range(heads):
-                mine = slice(head * HEAD_DIM, (head + 1) * HEAD_DIM)
+
+            def one_head(head):
+                mine = pl.ds(pl.multiple_of(head * HEAD_DIM, HEAD_DIM), HEAD_DIM)
                 scores = dot_nt(k_out[0:span, :], head_only(queries, head))
                 slot = lax.broadcasted_iota(jnp.int32, (span, BLOCK), 0)
                 scores = jnp.where(slot < length, scores, masked_score)
@@ -137,7 +158,9 @@
                 total = jnp.sum(weights, axis=0, keepdims=True)
                 result = dot_nn(values_t[mine, 0:span], weights.astype(bf16))
                 out_t[mine, :] = result * (1.0 / total)
-                log_sum[head : head + 1, rows] = top + jnp.log(total)
+                log_sum[pl.ds(head, 1), rows] = top + jnp.log(total)
+
+            head_pairs(heads, one_head)
             attended[rows, :] = out_t[...].T.astype(bf16)
             return carry
 
@@ -150,7 +173,8 @@
         rows = block_rows(block)
         row = attended[rows, :]
         for place in range(count):
-            part = dot_nt(row, weight[3, feature_block(index, place, width), :])
+            mine = chunk_block(index, place, width, chunk)
+            part = dot_nt(row, stacked(second_weight, chunk, chunk, mine))
             target = slice((place // 2) * width, (place // 2 + 1) * width)
             if place % 2:
                 send[rows, target] = part.astype(bf16)
@@ -164,14 +188,24 @@
 def mlp_kernel(place_ref, lengths, *refs, seq, count, width, slots, full):
     rows_in = refs[:count]
     grads_in = refs[count : 2 * count]
-    gain, weight = refs[2 * count : 2 * count + 2]
-    (normed, grads, mixed, grad_expanded, stats, out_keep, out_send, back_keep, back_send, kept) = (
-        refs[2 * count + 2 :]
-    )
+    gain, first_weight, second_weight = refs[2 * count : 2 * count + 3]
+    (normed, grads, mixed, grad_expanded, stats, out_keep, out_send, back_keep, back_send) = refs[
+        2 * count + 3 : 2 * count + 12
+    ]
+    kept, down = refs[2 * count + 12 :]
+    half = first_weight.shape[1] // 3
+    chunk = 2 * half
     index = place_ref[0]
     length = lengths[seq]
     block = pl.program_id(0)
     rows = block_rows(block)
+
+    @pl.when(block == 0)
+    def _():
+        for place in range(first_weight.shape[0]):
+            start = place * chunk
+            down[start : start + half, :] = first_weight[place, chunk : chunk + half, :]
+            down[start + half : start + chunk, :] = second_weight[place, chunk : chunk + half, :]
 
     @pl.when(block * BLOCK < length)
     def _():
@@ -185,9 +219,9 @@
             grads[:, here] = grad.astype(bf16)
         row = normed[...]
         grad = grads[...]
-        gate = dot_nn(row, weight[0])
-        linear = dot_nn(row, weight[1])
-        grad_mixed = dot_nn(grad, weight[2])
+        gate = dot_nn(row, stacked(first_weight, 0, chunk))
+        linear = dot_nn(row, stacked(second_weight, 0, chunk))
+        grad_mixed = dot_nn(grad, down[...])
         phi = 0.5 + 0.5 * lax.erf(gate * (0.5**0.5))
         activated = gate * phi
         density = jnp.exp(-0.5 * gate * gate) * (0.5 / jnp.pi) ** 0.5
@@ -202,8 +236,10 @@
         for place in range(count):
             here = feature_block(index, place, width)
             target = slice((place // 2) * width, (place // 2 + 1) * width)
-            part = dot_nt(mixed_low, weight[2, here, :])
-            back = dot_nt(first, weight[0, here, :]) + dot_nt(second, weight[1, here, :])
+            mine = chunk_block(index, place, width, chunk)
+            part = dot_nt(mixed_low, down[here, :])
+            back = dot_nt(first, stacked(first_weight, 0, chunk, mine))
+            back += dot_nt(second, stacked(second_weight, 0, chunk, mine))
             plain_sum += jnp.sum(back * gain[pl.ds(index ^ place, 1), :], axis=-1, keepdims=True)
             unit_sum += jnp.sum(back * normed[:, here].astype(f32), axis=-1, keepdims=True)
             if place % 2:
@@ -230,13 +266,15 @@
 
 def attend_back_kernel(place_ref, lengths, *refs, seq, count, width, heads, slots, full):
     grads_in = refs[:count]
-    (q_in, k_in, v_in, attended, log_sum, normed, gain, weight, cos_ref, low_ref, high_ref) = refs[
-        count : count + 11
+    q_in, k_in, v_in, attended, log_sum, normed, gain = refs[count : count + 7]
+    first_weight, second_weight, cos_ref, low_ref, high_ref = refs[count + 7 : count + 12]
+    grads, grad_projected, stats, keep, send = refs[count + 12 : count + 17]
+    (grad_att, delta, keys_t, probs_all, scores_all, query_t, key_total, value_total) = refs[
+        count + 17 : count + 25
     ]
-    grads, grad_projected, stats, keep, send = refs[count + 11 : count + 16]
-    (grad_att, delta, keys_t, probs_all, scores_all, query_t, key_total, value_total) = refs[
-        count + 16 :
-    ]
+    queries_all, grads_all = refs[count + 25 :]
+    chunk = first_weight.shape[1] // 2
+    places = ((first_weight, 0), (first_weight, chunk), (second_weight, 0))
     index = place_ref[0]
     length = lengths[seq]
     live = pl.cdiv(length, BLOCK)
@@ -246,7 +284,7 @@
         rows = block_rows(block)
         for place in range(count):
             grads[rows, feature_block(index, place, width)] = grads_in[place][rows, :]
-        grad = dot_nn(grads[rows, :], weight[3]).astype(bf16)
+        grad = dot_nn(grads[rows, :], stacked(second_weight, chunk, chunk)).astype(bf16)
         grad_att[rows, :] = grad
         inner = (grad.astype(f32) * attended[rows, :].astype(f32)).T
         for head in range(heads):
@@ -275,22 +313,27 @@
 
         def query_block(block, carry):
             rows = block_rows(block)
-            queries = [head_only(q_in[rows, :], head) for head in range(heads)]
-            grad_rows = [head_only(grad_att[rows, :], head) for head in range(heads)]
-            for head in range(heads):
-                mine = slice(head * HEAD_DIM, (head + 1) * HEAD_DIM)
-                lanes = slice(head * BLOCK, (head + 1) * BLOCK)
-                scores = dot_nt(k_in[0:span, :], queries[head])
+
+            def one_head(head):
+                mine = pl.ds(pl.multiple_of(head * HEAD_DIM, HEAD_DIM), HEAD_DIM)
+                lanes = pl.ds(pl.multiple_of(head * BLOCK, BLOCK), BLOCK)
+                queries = head_only(q_in[rows, :], head)
+                grad_rows = head_only(grad_att[rows, :], head)
+                queries_all[lanes, :] = queries
+                grads_all[lanes, :] = grad_rows
+                scores = dot_nt(k_in[0:span, :], queries)
                 slot = lax.broadcasted_iota(jnp.int32, (span, BLOCK), 0)
                 scores = jnp.where(slot < length, scores, masked_score)
-                weights = jnp.exp(scores - log_sum[head : head + 1, rows])
-                grad_weights = dot_nt(v_in[0:span, :], grad_rows[head])
-                grad_scores = (weights * (grad_weights - delta[head : head + 1, rows])).astype(bf16)
+                weights = jnp.exp(scores - log_sum[pl.ds(head, 1), rows])
+                grad_weights = dot_nt(v_in[0:span, :], grad_rows)
+                grad_scores = (weights * (grad_weights - delta[pl.ds(head, 1), rows])).astype(bf16)
                 probs_all[0:span, lanes] = weights.astype(bf16)
                 scores_all[0:span, lanes] = grad_scores
                 query_t[mine, :] = dot_nn(keys_t[mine, 0:span], grad_scores)
-            value_total[0:span, :] += dot_nn(probs_all[0:span, :], jnp.concatenate(grad_rows, axis=0))
-            key_total[0:span, :] += dot_nn(scores_all[0:span, :], jnp.concatenate(queries, axis=0))
+
+            head_pairs(heads, one_head)
+            value_total[0:span, :] += dot_nn(probs_all[0:span, :], grads_all[...])
+            key_total[0:span, :] += dot_nn(scores_all[0:span, :], queries_all[...])
             turned = turn(query_t[...].T * HEAD_DIM**-0.5, cos_ref, low_ref, high_ref, rows, -1.0)
             grad_projected[0, rows, :] = turned.astype(bf16)
             return carry
@@ -309,9 +352,11 @@
         unit_sum = jnp.zeros((BLOCK, 1), f32)
         for place in range(count):
             here = feature_block(index, place, width)
+            mine = chunk_block(index, place, width, chunk)
             target = slice((place // 2) * width, (place // 2 + 1) * width)
             back = sum(
-                dot_nt(grad_projected[kind, rows, :], weight[kind, here, :]) for kind in range(3)
+                dot_nt(grad_projected[kind, rows, :], stacked(ref, start, chunk, mine))
+                for kind, (ref, start) in enumerate(places)
             )
             plain_sum += jnp.sum(back * gain[pl.ds(index ^ place, 1), :], axis=-1, keepdims=True)
             unit_sum += jnp.sum(back * normed[rows, here].astype(f32), axis=-1, keepdims=True)
@@ -418,23 +463,27 @@
     gain_grad[0:1, :] += jnp.sum(gradient * unit, axis=0, keepdims=True)
 
 
-def grad_kernel(*refs, pairs, seq_count):
-    out = refs[-1]
-    place = 0
+def grad_kernel(*refs, pairs, seq_count, layout):
+    outs = refs[-2:]
     cursor = 0
+    pieces = iter(layout)
     for kinds in pairs:
         lefts = refs[cursor : cursor + seq_count]
         rights = refs[cursor + seq_count : cursor + 2 * seq_count]
         cursor += 2 * seq_count
         for kind in range(kinds):
             total = sum(dot_tn(left[...], right[kind]) for left, right in zip(lefts, rights))
-            for step in range(out.shape[0]):
-                rows = out.shape[2]
-                out[step, place] = total[step * rows : (step + 1) * rows, :].astype(bf16)
-            place += 1
-
-
-def weight_grads(groups, wide_count, full, micros, earlier):
+            moves = next(pieces)
+            rows = sum(size for _, _, size in moves)
+            for step in range(outs[0].shape[0]):
+                start = step * rows
+                for out, target, size in moves:
+                    part = total[start : start + size, :].astype(bf16)
+                    outs[out][step, target : target + size, :] = part
+                    start += size
+
+
+def weight_grads(groups, layout, wide_count, full, micros, earlier):
     rows = full // wide_count
     per_step = max(BLOCK // rows, 1)
     columns = groups[0][1][0].shape[2]
@@ -450,15 +499,15 @@
         for right in rights:
             operands.append(right)
             specs.append(pl.BlockSpec(right.shape, lambda step: (0, 0, 0)))
-    kinds = sum(pairs)
-    body = functools.partial(grad_kernel, pairs=pairs, seq_count=seq_count)
+    lines = sum(pairs) * rows // 2
+    body = functools.partial(grad_kernel, pairs=pairs, seq_count=seq_count, layout=layout)
     body, operands, specs = after(body, operands, specs, earlier, 0)
     return pl.pallas_call(
         body,
         grid=(wide_count // per_step,),
         in_specs=specs,
-        out_specs=pl.BlockSpec((per_step, kinds, rows, columns), lambda step: (step, 0, 0, 0)),
-        out_shape=jax.ShapeDtypeStruct((wide_count, kinds, rows, columns), bf16),
+        out_specs=[pl.BlockSpec((per_step, lines, columns), lambda step: (step, 0, 0))] * 2,
+        out_shape=[jax.ShapeDtypeStruct((wide_count, lines, columns), bf16)] * 2,
         cost_estimate=estimate(micros),
     )(*operands)
 
@@ -568,14 +617,59 @@
     return [term for term, _ in terms], sums
 
 
+def swap_wide(values, bit, wide_count):
+    return lax.ppermute(values, "wide", [(at, at ^ (1 << bit)) for at in range(wide_count)])
+
+
+def bit_orders(wide_count):
+    bits = wide_count.bit_length() - 1
+    first = list(range(bits))
+    return first, first[1::-1] + first[2:]
+
+
+def gather_wide(parts, wide_count):
+    bits = wide_count.bit_length() - 1
+    index = lax.axis_index("wide")
+    mine = [(index >> bit) & 1 for bit in range(bits)]
+    zero = jnp.zeros((), mine[0].dtype)
+    whole_parts = []
+    for part in parts:
+        space = jnp.zeros((2,) * bits + part.shape, part.dtype)
+        start = mine[::-1] + [zero, zero]
+        whole_parts.append(lax.dynamic_update_slice(space, part.reshape((1,) * bits + part.shape), start))
+    for stage in range(bits):
+        moved = []
+        for place, order in enumerate(bit_orders(wide_count)):
+            done = order[::-1][:stage]
+            start = [zero if bit in done else mine[bit] for bit in range(bits)][::-1]
+            sizes = [2 if bit in done else 1 for bit in range(bits)][::-1]
+            going = lax.dynamic_slice(
+                whole_parts[place], start + [zero, zero], sizes + list(parts[place].shape)
+            )
+            bit = order[::-1][stage]
+            received = swap_wide(going, bit, wide_count)
+            start[bits - 1 - bit] = 1 - mine[bit]
+            moved.append((received, start))
+        for place, (received, start) in enumerate(moved):
+            whole_parts[place] = lax.dynamic_update_slice(
+                whole_parts[place], received, start + [zero, zero]
+            )
+    return [
+        space.reshape((wide_count,) + part.shape) for space, part in zip(whole_parts, parts)
+    ]
+
+
+def sum_wide(values, wide_count):
+    for bit in range(wide_count.bit_length() - 1):
+        values = values + swap_wide(values, bit, wide_count)
+    return values
+
+
 def reduce_wide(parts, wide_count):
     bits = wide_count.bit_length() - 1
     index = lax.axis_index("wide")
     states = []
-    for place, part in enumerate(parts):
-        order = list(range(bits))
-        if place % 2 and bits > 1:
-            order[0], order[1] = order[1], order[0]
+    for part, order in zip(parts, bit_orders(wide_count)):
         states.append((part.reshape((2,) * bits + part.shape[1:]), order, list(range(bits))[::-1]))
     for stage in range(bits):
         moved = []
@@ -584,9 +678,7 @@
             axis = axes.index(bit)
             mine = (index >> bit) & 1
             going = lax.dynamic_index_in_dim(part, 1 - mine, axis, keepdims=False)
-            received = lax.ppermute(
-                going, "wide", [(at, at ^ (1 << bit)) for at in range(wide_count)]
-            )
+            received = swap_wide(going, bit, wide_count)
             moved.append((axis, mine, received))
         for place, (axis, mine, received) in enumerate(moved):
             part, order, axes = states[place]
@@ -640,11 +732,22 @@
     blocks = slots // GLUE
     meta = (index.reshape(1), lengths)
 
-    attn_weight = lax.all_gather(
-        jnp.concatenate([attn_in_weight, attn_out_weight.T[None]]), "wide", axis=1, tiled=True
+    rows = full // wide_count
+    out_turned = attn_out_weight.T
+    attn_weights = gather_wide(
+        [
+            attn_in_weight[:2].reshape(2 * rows, width),
+            jnp.concatenate([attn_in_weight[2], out_turned]),
+        ],
+        wide_count,
     )
-    mlp_weight = lax.all_gather(
-        jnp.concatenate([mlp_in_weight, mlp_out_weight.T[None]]), "wide", axis=1, tiled=True
+    down_turned = mlp_out_weight.T
+    mlp_weights = gather_wide(
+        [
+            jnp.concatenate([mlp_in_weight[0], down_turned[: rows // 2]]),
+            jnp.concatenate([mlp_in_weight[1], down_turned[rows // 2 :]]),
+        ],
+        wide_count,
     )
     input_pieces = gather_narrow(inputs, count)
     grad_pieces = gather_narrow(cotangent, count)
@@ -657,15 +760,16 @@
     row_spec = whole((slots, width))
     table_specs = [whole((slots, 128))] * 3
     gain_spec = whole((count, width))
-    attn_spec = whole(attn_weight.shape)
+    attn_specs = [whole(part.shape) for part in attn_weights]
+    mlp_specs = [whole(part.shape) for part in mlp_weights]
     sizes = dict(count=count, width=width, slots=slots, full=full)
 
     def forward_call(seq, earlier):
         return call_kernel(
             functools.partial(attend_kernel, seq=seq, heads=heads, **sizes),
             meta,
-            [*input_pieces, attn_gain_rows, attn_weight, *tables],
-            [seq_spec(seq)] * count + [gain_spec, attn_spec] + table_specs,
+            [*input_pieces, attn_gain_rows, *attn_weights, *tables],
+            [seq_spec(seq)] * count + [gain_spec] + attn_specs + table_specs,
             [((slots, full), bf16)]
             + [((slots, width), bf16)] * 4
             + [((max(heads, STAT_ROWS), slots), f32), ((STAT_ROWS, slots), f32)]
@@ -679,15 +783,16 @@
         return call_kernel(
             functools.partial(mlp_kernel, seq=seq, **sizes),
             meta,
-            [*residual_pieces[seq], *grad_pieces, mlp_gain_rows, mlp_weight],
+            [*residual_pieces[seq], *grad_pieces, mlp_gain_rows, *mlp_weights],
             [striped(width, rows=BLOCK)] * count
             + [striped(width, seq, slots // BLOCK, rows=BLOCK)] * count
-            + [gain_spec, whole(mlp_weight.shape)],
+            + [gain_spec]
+            + mlp_specs,
             [((slots, full), bf16), ((slots, full), bf16), ((slots, hidden), bf16)]
             + [((2, slots, hidden), bf16), ((STAT_ROWS, slots), f32)]
             + [((slots, half), bf16)] * 3
             + [((slots + TAIL, half), bf16)],
-            [pltpu.VMEM((STAT_ROWS, slots), f32)],
+            [pltpu.VMEM((STAT_ROWS, slots), f32), pltpu.VMEM((full, hidden), bf16)],
             20,
             earlier,
             slots // BLOCK,
@@ -705,9 +810,10 @@
             functools.partial(attend_back_kernel, seq=seq, heads=heads, **sizes),
             meta,
             [*attn_grad_pieces[seq], queries, keys, values, attended, log_sum, normed]
-            + [attn_gain_rows, attn_weight, *tables],
+            + [attn_gain_rows, *attn_weights, *tables],
             [row_spec] * (count + 4)
-            + [whole(log_sum.shape), whole((slots, full)), gain_spec, attn_spec]
+            + [whole(log_sum.shape), whole((slots, full)), gain_spec]
+            + attn_specs
             + table_specs,
             [((slots, full), bf16), ((3, slots, width), bf16), ((STAT_ROWS, slots), f32)]
             + [((slots, half), bf16), ((slots + TAIL, half), bf16)],
@@ -720,6 +826,8 @@
                 pltpu.VMEM((width, BLOCK), f32),
                 pltpu.VMEM((slots, width), f32),
                 pltpu.VMEM((slots, width), f32),
+                pltpu.VMEM((heads * BLOCK, width), bf16),
+                pltpu.VMEM((heads * BLOCK, width), bf16),
             ],
             26,
             earlier,
@@ -791,17 +899,16 @@
             ([middle[seq][0] for seq in seqs], [middle[seq][3] for seq in seqs]),
             ([middle[seq][1] for seq in seqs], [middle[seq][2][None] for seq in seqs]),
         ],
+        (((0, 0, rows),), ((1, 0, rows),), ((0, rows, rows // 2), (1, rows, rows // 2))),
         wide_count,
         full,
         17,
         earlier,
     )
-    mlp_shard = lax.psum_scatter(
-        mlp_grads.reshape(-1, hidden), "wide", scatter_dimension=0, tiled=True
-    )
+    mlp_first, mlp_second = reduce_wide(mlp_grads, wide_count)
 
     backward, output, inputs_grad = [], [], []
-    earlier = [mlp_grads]
+    earlier = [mlp_grads[0]]
     for seq in seqs:
         backward.append(backward_call(seq, earlier))
         earlier = [backward[seq][2]]
@@ -822,22 +929,13 @@
             ([forward[seq][0] for seq in seqs], [backward[seq][1] for seq in seqs]),
             ([backward[seq][0] for seq in seqs], [forward[seq][4][None] for seq in seqs]),
         ],
+        (((0, 0, rows),), ((0, rows, rows),), ((1, 0, rows),), ((1, rows, rows),)),
         wide_count,
         full,
         10,
         earlier,
     )
-    mlp_shard = mlp_shard.reshape(mlp_grads.shape[1:])
-    kinds, rows = attn_grads.shape[1:3]
-    attn_shard = jnp.concatenate(
-        reduce_wide(
-            [
-                attn_grads[:, start : start + kinds // 2].reshape(wide_count, -1, width)
-                for start in range(0, kinds, kinds // 2)
-            ],
-            wide_count,
-        )
-    ).reshape(kinds, rows, width)
+    attn_first, attn_second = reduce_wide(attn_grads, wide_count)
 
     attn_gain_local = 0.0
     for seq in seqs:
@@ -853,18 +951,16 @@
             inputs_grad,
         )
         attn_gain_local = attn_gain_local + gain_part[0]
-    gain_grads = jnp.sum(
-        lax.all_gather(jnp.stack([attn_gain_local, mlp_gain_local]), "wide"), axis=0
-    )
+    gain_grads = sum_wide(jnp.stack([attn_gain_local, mlp_gain_local]), wide_count)
     return (
         output[0],
         inputs_grad[0],
         gain_grads[0],
-        attn_shard[:3],
-        attn_shard[3].T,
+        jnp.stack([attn_first[:rows], attn_first[rows:], attn_second[:rows]]),
+        attn_second[rows:].T,
         gain_grads[1],
-        mlp_shard[:2].astype(f32),
-        mlp_shard[2].T.astype(f32),
+        jnp.stack([mlp_first[:rows], mlp_second[:rows]]),
+        jnp.concatenate([mlp_first[rows:], mlp_second[rows:]]).T,
     )
 
 

time: 470 us -> 514 us (1.094)
  local copies, waits for them, and re-layouts: 25.1 us -> 71.3 us
  starting transfers between devices: 25.1 us -> 52.9 us
  blocking collectives: 26.1 us -> 0 us
  between operations: 14.6 us -> 1.79 us
  Pallas kernels: 222 us -> 228 us
    ppermute x6 -> x27, waiting for transfers between devices: 36.4 us -> 67.2 us  [swap_wide(): lax.ppermute(values, 'wide', [(at, at ^ 1 << bit) for at in range(wide_co...]
    ppermute x6 -> x27, starting transfers between devices: 3.88 us -> 33.6 us  [swap_wide(): lax.ppermute(values, 'wide', [(at, at ^ 1 << bit) for at in range(wide_co...]
    ppermute x34, waiting for transfers between devices: 99.6 us -> 71.3 us  [swap(): lax.ppermute(values, 'narrow', [(place, place ^ distance) for place in ra...]
    all_gather x1 -> x0, blocking collectives: 26.1 us -> none  [shards(): lax.all_gather(jnp.stack([attn_gain_local, mlp_gain_local]), 'wide')]
    dynamic_update_slice x0 -> x16, local copies, waits for them, and re-layouts: none -> 16.3 us  [the longest x12 15.5 us: gather_wide(): lax.dynamic_update_slice(whole_parts[place], received, start + [zero, zero])]
    dynamic_slice x0 -> x12, local copies, waits for them, and re-layouts: none -> 14.2 us  [gather_wide(): lax.dynamic_slice(whole_parts[place], start + [zero, zero], sizes + list(...]
    pallas_call x6, Pallas kernels: 141 us -> 148 us  [call_kernel(): pl.pallas_call(body, grid_spec=pltpu.PrefetchScalarGridSpec(num_scalar_pr...]
    unnamed x56 -> x48, local copies, waits for them, and re-layouts: 16.2 us -> 9.9 us
  transfers between devices with their start and end apart: 43 -> 61, of which waited for: 16 -> 25; matrix products, arithmetic and copies ran while one was open for 3% -> 14% of each run, Pallas kernels for 48% -> 29%
where the time goes in v1:
time: 514 us; the launch traced here: 505 us
  Pallas kernels  228 us (44%)
  waiting for transfers between devices  138 us (27%)
  local copies, waits for them, and re-layouts  71.3 us (14%)
  starting transfers between devices  52.9 us (10%)
  other arithmetic  12.1 us (2%)
    pallas_call x6, Pallas kernels, call_kernel(): pl.pallas_call(body, grid_spec=pltpu.PrefetchScalarGridSpec(num_scalar_pr...  148 us
    ppermute x34, waiting for transfers between devices, swap(): lax.ppermute(values, 'narrow', [(place, place ^ distance) for place in ra...  71.3 us
    ppermute x27, waiting for transfers between devices, swap_wide(): lax.ppermute(values, 'wide', [(at, at ^ 1 << bit) for at in range(wide_co...  67.2 us
    pallas_call x16, Pallas kernels, glue_call(): pl.pallas_call(body, grid_spec=pltpu.PrefetchScalarGridSpec(num_scalar_pr...  45.7 us
    pallas_call x2, Pallas kernels, weight_grads(): pl.pallas_call(body, grid=(wide_count // per_step,), in_specs=specs, out_...  34.1 us
    ppermute x27, starting transfers between devices, swap_wide(): lax.ppermute(values, 'wide', [(at, at ^ 1 << bit) for at in range(wide_co...  33.6 us
    ppermute x34, starting transfers between devices, swap(): lax.ppermute(values, 'narrow', [(place, place ^ distance) for place in ra...  19.3 us
    dynamic_update_slice x12, local copies, waits for them, and re-layouts, gather_wide(): lax.dynamic_update_slice(whole_parts[place], received, start + [zero, zero])  15.5 us
  transfers between devices with their start and end apart: 61, of which 25 were waited for; matrix products, arithmetic and copies ran while one was open for 14% of the time, Pallas kernels for 29%

profile of v1, /device:TPU:0, one launch (start us, length us, event | category | flops | bytes accessed | tf_op | source)
XLA Modules:
  0.0 504.6 jit_solution(13834893491963769477)
XLA Ops:
  39.8 5.9 %collective-permute-done.17 = bf16[1,1,1,192,656]{4,3,2,1,0:T(8,128)(2,1)} collective-permute-done((bf16[1,1,1,192,656]{4,3,2,1,0:T(8,128)(2,1)}, bf16[1,1,1,192,656]{4,3,2,1,0:T(8,128)(2,1)}, u32[]{:S(2)}, u32[]{:S(2)}) %collective-permute-start.17) | collective-permute-done | bytes 251936 | tf_op jit(solution)/shard_map/ppermute | solution.py:621
  71.6 26.4 %shard_map.152 = (bf16[1024,1024]{1,0:T(8,128)(2,1)}, bf16[1024,256]{1,0:T(8,128)(2,1)}, bf16[1024,256]{1,0:T(8,128)(2,1)}, bf16[1024,256]{1,0:T(8,128)(2,1)}, b...) custom-call(s32[1]{0:T(128)} %bitcast.refs_0_.place_ref, ...), custom_call_target="tpu_custom_call" | custom-call | flops 24000000000 | bytes 1048576 | tf_op jit(solution)/shard_map/pallas_call | solution.py:557
  98.0 26.6 %shard_map.153 = (bf16[1024,1024]{1,0:T(8,128)(2,1)}, bf16[1024,256]{1,0:T(8,128)(2,1)}, bf16[1024,256]{1,0:T(8,128)(2,1)}, bf16[1024,256]{1,0:T(8,128)(2,1)}, b...) custom-call(s32[1]{0:T(128)} %bitcast.refs_0_.place_ref, ...), custom_call_target="tpu_custom_call" | custom-call | flops 24000000000 | bytes 1048576 | tf_op jit(solution)/shard_map/pallas_call | solution.py:557
  132.5 9.9 %collective-permute-done.21 = bf16[2,1,1,192,656]{4,3,2,1,0:T(8,128)(2,1)S(1)} collective-permute-done((bf16[2,1,1,192,656]{4,3,2,1,0:T(8,128)(2,1)S(1)}, bf16[2,1,1,192,656]{4,3,2,1,0:T(8,128)(2,1)S(1)}, u32[]{:S(2)}, u32[]{:S(2)}) %collective-permute-start.21) | collective-permute-done | bytes 503840 | tf_op jit(solution)/shard_map/ppermute | solution.py:621
  151.0 8.7 %collective-permute-done.24.refs_2_ = bf16[1024,256]{1,0:T(8,128)(2,1)} collective-permute-done((bf16[1024,256]{1,0:T(8,128)(2,1)}, bf16[1024,256]{1,0:T(8,128)(2,1)}, u32[]{:S(2)}, u32[]{:S(2)}) %collective-permute-start.24) | collective-permute-done | bytes 524320 | tf_op jit(solution)/shard_map/ppermute | solution.py:572
  162.2 5.9 %collective-permute-done.11.refs_2_ = bf16[1024,256]{1,0:T(8,128)(2,1)} collective-permute-done((bf16[1024,256]{1,0:T(8,128)(2,1)}, bf16[1024,256]{1,0:T(8,128)(2,1)}, u32[]{:S(2)}, u32[]{:S(2)}) %collective-permute-start.11) | collective-permute-done | bytes 524320 | tf_op jit(solution)/shard_map/ppermute | solution.py:572
  175.6 7.7 %collective-permute-done.26.refs_4_ = bf16[1024,256]{1,0:T(8,128)(2,1)} collective-permute-done((bf16[1024,256]{1,0:T(8,128)(2,1)}, bf16[1024,256]{1,0:T(8,128)(2,1)}, u32[]{:S(2)}, u32[]{:S(2)}) %collective-permute-start.26) | collective-permute-done | bytes 524320 | tf_op jit(solution)/shard_map/ppermute | solution.py:572
  190.9 20.4 %shard_map.158 = (bf16[1024,1024]{1,0:T(8,128)(2,1)}, bf16[1024,1024]{1,0:T(8,128)(2,1)}, bf16[1024,656]{1,0:T(8,128)(2,1)}, bf16[2,1024,656]{2,1,0:T(8,128)(2,1...) custom-call(s32[1]{0:T(128)} %bitcast.refs_0_.place_ref, ...), custom_call_target="tpu_custom_call" | custom-call | flops 20000000000 | bytes 1048576 | tf_op jit(solution)/shard_map/pallas_call | solution.py:557
  212.4 20.4 %shard_map.159 = (bf16[1024,1024]{1,0:T(8,128)(2,1)}, bf16[1024,1024]{1,0:T(8,128)(2,1)}, bf16[1024,656]{1,0:T(8,128)(2,1)}, bf16[2,1024,656]{2,1,0:T(8,128)(2,1...) custom-call(s32[1]{0:T(128)} %bitcast.refs_0_.place_ref, ...), custom_call_target="tpu_custom_call" | custom-call | flops 20000000000 | bytes 1048576 | tf_op jit(solution)/shard_map/pallas_call | solution.py:557
  232.8 24.8 %shard_map.168 = (bf16[8,192,656]{2,1,0:T(8,128)(2,1)}, bf16[8,192,656]{2,1,0:T(8,128)(2,1)}) custom-call(bf16[1024,1024]{1,0:T(8,128)(2,1)} %get-tuple-element.118.refs_0_, bf16[1024,1024]{1,0:T(8,128)(2,1)} %get-tuple-element.119.refs_1_, bf16[2,1024,656]{2,1,0:T(8,128)(2,1)} %get-tuple-element.120.refs_2_, ...), custom_call_target="tpu_custom_call" | custom-call | flops 16999999488 | bytes 1048576 | tf_op jit(solution)/shard_map/pallas_call | solution.py:505
  263.1 24.4 %collective-permute-done.55 = bf16[2,2,192,656]{3,2,1,0:T(8,128)(2,1)S(1)} collective-permute-done((bf16[2,2,192,656]{3,2,1,0:T(8,128)(2,1)S(1)}, bf16[2,2,192,656]{3,2,1,0:T(8,128)(2,1)S(1)}, u32[]{:S(2)}, u32[]{:S(2)}) %collective-permute-start.55) | collective-permute-done | bytes 1007648 | tf_op jit(solution)/shard_map/ppermute | solution.py:621
  315.0 17.9 %collective-permute-done.38.refs_2_.refs_3_ = bf16[1040,256]{1,0:T(8,128)(2,1)} collective-permute-done((bf16[1040,256]{1,0:T(8,128)(2,1)}, bf16[1040,256]{1,0:T(8,128)(2,1)}, u32[]{:S(2)}, u32[]{:S(2)}) %collective-permute-start.38) | collective-permute-done | bytes 532512 | tf_op jit(solution)/shard_map/ppermute | solution.py:572
  332.9 4.4 shard_map.167
  344.3 4.4 shard_map.165
  351.0 4.6 collective-permute-done.40.refs_4_
  356.7 9.1 %collective-permute-done.35.refs_4_ = bf16[1024,256]{1,0:T(8,128)(2,1)} collective-permute-done((bf16[1024,256]{1,0:T(8,128)(2,1)}, bf16[1024,256]{1,0:T(8,128)(2,1)}, u32[]{:S(2)}, u32[]{:S(2)}) %collective-permute-start.35) | collective-permute-done | bytes 524320 | tf_op jit(solution)/shard_map/ppermute | solution.py:572
  365.8 27.1 %shard_map.169 = (bf16[1024,1024]{1,0:T(8,128)(2,1)}, bf16[3,1024,256]{2,1,0:T(8,128)(2,1)}, f32[8,1024]{1,0:T(8,128)}, bf16[1024,512]{1,0:T(8,128)(2,1)}, bf16[1040,512]{1,0:T(8,128)(2,1)}) custom-call(s32[1]{0:T(128)} %bitcast.refs_0_.place_ref, s32[2]{0:T(128)} %lengths.11, bf16[1024,256]{1,0:T(8,128)(2,1)} %get-tuple-element.111.refs_2_, ...), custom_call_target="tpu_custom_call" | custom-call | flops 25999998976 | bytes 1048576 | tf_op jit(solution)/shard_map/pallas_call | solution.py:557
  393.8 27.3 %shard_map.170 = (bf16[1024,1024]{1,0:T(8,128)(2,1)}, bf16[3,1024,256]{2,1,0:T(8,128)(2,1)}, f32[8,1024]{1,0:T(8,128)}, bf16[1024,512]{1,0:T(8,128)(2,1)}, bf16[1040,512]{1,0:T(8,128)(2,1)}) custom-call(s32[1]{0:T(128)} %bitcast.refs_0_.place_ref, s32[2]{0:T(128)} %lengths.11, bf16[1024,256]{1,0:T(8,128)(2,1)} %get-tuple-element.100.refs_2_, ...), custom_call_target="tpu_custom_call" | custom-call | flops 25999998976 | bytes 1048576 | tf_op jit(solution)/shard_map/pallas_call | solution.py:557
  421.0 9.4 %shard_map.175 = (bf16[8,256,256]{2,1,0:T(8,128)(2,1)}, bf16[8,256,256]{2,1,0:T(8,128)(2,1)}) custom-call(bf16[1024,1024]{1,0:T(8,128)(2,1)} %get-tuple-element.117.refs_11_.refs_0_, bf16[1024,1024]{1,0:T(8,128)(2,1)} %get-tuple-element.106.refs_11_.refs_1_, bf16[3,1024,256]{2,1,0:T(8,128)(2,1)} %get-tuple-element.145.refs_2_, ...), custom_call_target="tpu_custom_call" | custom-call | flops 10000000000 | bytes 1048576 | tf_op jit(solution)/shard_map/pallas_call | solution.py:505
  440.7 6.6 %collective-permute-done.52 = bf16[2,2,256,256]{2,3,0,1:T(8,128)(2,1)} collective-permute-done((bf16[2,2,256,256]{2,3,0,1:T(8,128)(2,1)}, bf16[2,2,256,256]{2,3,0,1:T(8,128)(2,1)}, u32[]{:S(2)}, u32[]{:S(2)}) %collective-permute-start.52) | collective-permute-done | bytes 524320 | tf_op jit(solution)/shard_map/ppermute | solution.py:621
  456.6 4.3 collective-permute-done.50
  470.2 8.1 %collective-permute-done.45.refs_2_.refs_3_ = bf16[1040,256]{1,0:T(8,128)(2,1)S(1)} collective-permute-done((bf16[1040,256]{1,0:T(8,128)(2,1)}, bf16[1040,256]{1,0:T(8,128)(2,1)S(1)}, u32[]{:S(2)}, u32[]{:S(2)}) %collective-permute-start.45) | collective-permute-done | bytes 532512 | tf_op jit(solution)/shard_map/ppermute | solution.py:572
  479.2 4.3 shard_map.173
  486.7 4.3 shard_map.174
  (266 shorter events, 190.0 us)
Async XLA Ops:
  0.6 33.1 %collective-permute-start.1 = (bf16[2048,256]{1,0:T(8,128)(2,1)}, bf16[2048,256]{1,0:T(8,128)(2,1)}, u32[]{:S(2)}, u32[]{:S(2)}) collective-permute-start(bf16[2048,256]{1,0:T(8,128)(2,1)} %refs_6_.7), channel_id=1, source_target_pairs={{0,2},{1,3},{2,0},{3,1},{4,6},{5,7},{6,4},{7,5},{8,10},{9,11},{10,... | collective-permute-start | bytes 3145736 | tf_op jit(solution)/shard_map/ppermute | solution.py:572
  3.7 67.9 %collective-permute-start = (bf16[2048,256]{1,0:T(8,128)(2,1)}, bf16[2048,256]{1,0:T(8,128)(2,1)}, u32[]{:S(2)}, u32[]{:S(2)}) collective-permute-start(bf16[2048,256]{1,0:T(8,128)(2,1)} %refs_6_.7), channel_id=1, source_target_pairs={{0,1},{1,0},{2,3},{3,2},{4,5},{5,4},{6,7},{7,6},{8,9},{9,8},{10,11... | collective-permute-start | bytes 3145736 | tf_op jit(solution)/shard_map/ppermute | solution.py:572
  12.7 58.9 %collective-permute-start.9 = (bf16[2048,256]{1,0:T(8,128)(2,1)}, bf16[2048,256]{1,0:T(8,128)(2,1)}, u32[]{:S(2)}, u32[]{:S(2)}) collective-permute-start(bf16[2048,256]{1,0:T(8,128)(2,1)} %refs_7_.3), channel_id=1, source_target_pairs={{0,2},{1,3},{2,0},{3,1},{4,6},{5,7},{6,4},{7,5},{8,10},{9,11},{10,... | collective-permute-start | bytes 3145736 | tf_op jit(solution)/shard_map/ppermute | solution.py:572
  33.7 37.9 %collective-permute-start.2 = (bf16[2048,256]{1,0:T(8,128)(2,1)}, bf16[2048,256]{1,0:T(8,128)(2,1)}, u32[]{:S(2)}, u32[]{:S(2)}) collective-permute-start(bf16[2048,256]{1,0:T(8,128)(2,1)} %collective-permute-done.1.refs_4_), channel_id=1, source_target_pairs={{0,1},{1,0},{2,3},{3,2},{4,5},{5,4},{6,7},{7,6},{8,9},{9,8},{10,11... | collective-permute-start | bytes 3145736 | tf_op jit(solution)/shard_map/ppermute | solution.py:572
  34.7 30.2 %collective-permute-start.5 = (bf16[2,2,1,256,256]{4,3,2,1,0:T(8,128)(2,1)}, bf16[2,2,1,256,256]{4,3,2,1,0:T(8,128)(2,1)}, u32[]{:S(2)}, u32[]{:S(2)}) collective-permute-start(bf16[2,2,1,256,256]{4,3,2,1,0:T(8,128)(2,1)} %constant_dynamic-slice_fusion.14), channel_id=1, source_target_pairs={{0,4},{4,0},{8,12},{12,8},{16,20},{20,16},{24,28},{28,24},{1,5},{5... | collective-permute-start | bytes 1572872 | tf_op jit(solution)/shard_map/ppermute | solution.py:621
  64.9 60.2 %collective-permute-start.20 = (bf16[1,1,1,192,656]{4,3,2,1,0:T(8,128)(2,1)}, bf16[1,1,1,192,656]{4,3,2,1,0:T(8,128)(2,1)}, u32[]{:S(2)}, u32[]{:S(2)}) collective-permute-start(bf16[1,1,1,192,656]{4,3,2,1,0:T(8,128)(2,1)} %constant_dynamic-slice_fusion.7), channel_id=1, source_target_pairs={{0,16},{4,20},{8,24},{12,28},{16,0},{20,4},{24,8},{28,12},{1,17},{... | collective-permute-start | bytes 755720 | tf_op jit(solution)/shard_map/ppermute | solution.py:621
  69.4 56.9 %collective-permute-start.18 = (bf16[2,1,1,192,656]{4,3,2,1,0:T(8,128)(2,1)}, bf16[2,1,1,192,656]{4,3,2,1,0:T(8,128)(2,1)}, u32[]{:S(2)}, u32[]{:S(2)}) collective-permute-start(bf16[2,1,1,192,656]{4,3,2,1,0:T(8,128)(2,1)} %constant_dynamic-slice_fusion.9), channel_id=1, source_target_pairs={{0,8},{4,12},{8,0},{12,4},{16,24},{20,28},{24,16},{28,20},{1,9},{5... | collective-permute-start | bytes 1511432 | tf_op jit(solution)/shard_map/ppermute | solution.py:621
  98.0 44.5 %collective-permute-start.23 = (bf16[1024,512]{1,0:T(8,128)(2,1)}, bf16[1024,512]{1,0:T(8,128)(2,1)}, u32[]{:S(2)}, u32[]{:S(2)}) collective-permute-start(bf16[1024,512]{1,0:T(8,128)(2,1)} %get-tuple-element.86), channel_id=1, source_target_pairs={{0,1},{1,0},{2,3},{3,2},{4,5},{5,4},{6,7},{7,6},{8,9},{9,8},{10,11... | collective-permute-start | bytes 3145736 | tf_op jit(solution)/shard_map/ppermute | solution.py:572
  130.5 41.6 %collective-permute-start.19 = (bf16[2,2,1,192,656]{4,3,2,1,0:T(8,128)(2,1)}, bf16[2,2,1,192,656]{4,3,2,1,0:T(8,128)(2,1)S(1)}, u32[]{:S(2)}, u32[]{:S(2)}) collective-permute-start(bf16[2,2,1,192,656]{4,3,2,1,0:T(8,128)(2,1)} %constant_dynamic-slice_fusion.8), channel_id=1, source_target_pairs={{0,4},{4,0},{8,12},{12,8},{16,20},{20,16},{24,28},{28,24},{1,5},{5... | collective-permute-start | bytes 3022856 | tf_op jit(solution)/shard_map/ppermute | solution.py:621
  150.9 35.4 %collective-permute-start.15 = (bf16[2048,256]{1,0:T(8,128)(2,1)}, bf16[2048,256]{1,0:T(8,128)(2,1)}, u32[]{:S(2)}, u32[]{:S(2)}) collective-permute-start(bf16[2048,256]{1,0:T(8,128)(2,1)} %refs_7_.3), channel_id=1, source_target_pairs={{0,1},{1,0},{2,3},{3,2},{4,5},{5,4},{6,7},{7,6},{8,9},{9,8},{10,11... | collective-permute-start | bytes 3145736 | tf_op jit(solution)/shard_map/ppermute | solution.py:572
  159.7 31.2 %collective-permute-start.16 = (bf16[2048,256]{1,0:T(8,128)(2,1)}, bf16[2048,256]{1,0:T(8,128)(2,1)}, u32[]{:S(2)}, u32[]{:S(2)}) collective-permute-start(bf16[2048,256]{1,0:T(8,128)(2,1)} %collective-permute-done.9.refs_12_.refs_8_), channel_id=1, source_target_pairs={{0,1},{1,0},{2,3},{3,2},{4,5},{5,4},{6,7},{7,6},{8,9},{9,8},{10,11... | collective-permute-start | bytes 3145736 | tf_op jit(solution)/shard_map/ppermute | solution.py:572
  259.1 28.4 %collective-permute-start.55 = (bf16[2,2,192,656]{3,2,1,0:T(8,128)(2,1)S(1)}, bf16[2,2,192,656]{3,2,1,0:T(8,128)(2,1)S(1)}, u32[]{:S(2)}, u32[]{:S(2)}) collective-permute-start(bf16[2,2,192,656]{3,2,1,0:T(8,128)(2,1)S(1)} %dynamic-slice_bitcast_fusion.1), channel_id=1, source_target_pairs={{0,4},{4,0},{8,12},{12,8},{16,20},{20,16},{24,28},{28,24},{1,5},{5... | collective-permute-start | bytes 3022856 | tf_op jit(solution)/shard_map/ppermute | solution.py:621
  259.7 29.2 %collective-permute-start.58 = (bf16[2,2,192,656]{3,2,1,0:T(8,128)(2,1)S(1)}, bf16[2,2,192,656]{3,2,1,0:T(8,128)(2,1)S(1)}, u32[]{:S(2)}, u32[]{:S(2)}) collective-permute-start(bf16[2,2,192,656]{3,2,1,0:T(8,128)(2,1)S(1)} %get-tuple-element.176), channel_id=1, source_target_pairs={{0,8},{4,12},{8,0},{12,4},{16,24},{20,28},{24,16},{28,20},{1,9},{5... | collective-permute-start | bytes 3022856 | tf_op jit(solution)/shard_map/ppermute | solution.py:621
  262.6 29.3 %collective-permute-start.30 = (bf16[1024,512]{1,0:T(8,128)(2,1)S(1)}, bf16[1024,512]{1,0:T(8,128)(2,1)}, u32[]{:S(2)}, u32[]{:S(2)}) collective-permute-start(bf16[1024,512]{1,0:T(8,128)(2,1)S(1)} %copy-done.16), channel_id=1, source_target_pairs={{0,1},{1,0},{2,3},{3,2},{4,5},{5,4},{6,7},{7,6},{8,9},{9,8},{10,11... | collective-permute-start | bytes 3145736 | tf_op jit(solution)/shard_map/ppermute | solution.py:572
  262.6 32.6 %collective-permute-start.28 = (bf16[1024,512]{1,0:T(8,128)(2,1)}, bf16[1024,512]{1,0:T(8,128)(2,1)S(1)}, u32[]{:S(2)}, u32[]{:S(2)}) collective-permute-start(bf16[1024,512]{1,0:T(8,128)(2,1)} %get-tuple-element.91), channel_id=1, source_target_pairs={{0,1},{1,0},{2,3},{3,2},{4,5},{5,4},{6,7},{7,6},{8,9},{9,8},{10,11... | collective-permute-start | bytes 3145736 | tf_op jit(solution)/shard_map/ppermute | solution.py:572
  263.1 35.6 %collective-permute-start.37 = (bf16[1040,512]{1,0:T(8,128)(2,1)}, bf16[1040,512]{1,0:T(8,128)(2,1)}, u32[]{:S(2)}, u32[]{:S(2)}) collective-permute-start(bf16[1040,512]{1,0:T(8,128)(2,1)} %get-tuple-element.108), channel_id=1, source_target_pairs={{0,1},{1,0},{2,3},{3,2},{4,5},{5,4},{6,7},{7,6},{8,9},{9,8},{10,11... | collective-permute-start | bytes 3194888 | tf_op jit(solution)/shard_map/ppermute | solution.py:572
  298.7 40.2 %collective-permute-start.29 = (bf16[1024,256]{1,0:T(8,128)(2,1)}, bf16[1024,256]{1,0:T(8,128)(2,1)S(1)}, u32[]{:S(2)}, u32[]{:S(2)}) collective-permute-start(bf16[1024,256]{1,0:T(8,128)(2,1)} %shard_map.160), channel_id=1, source_target_pairs={{0,2},{1,3},{2,0},{3,1},{4,6},{5,7},{6,4},{7,5},{8,10},{9,11},{10,... | collective-permute-start | bytes 1572872 | tf_op jit(solution)/shard_map/ppermute | solution.py:572
  301.8 31.2 %collective-permute-start.38 = (bf16[1040,256]{1,0:T(8,128)(2,1)}, bf16[1040,256]{1,0:T(8,128)(2,1)}, u32[]{:S(2)}, u32[]{:S(2)}) collective-permute-start(bf16[1040,256]{1,0:T(8,128)(2,1)} %get-tuple-element.109), channel_id=1, source_target_pairs={{0,2},{1,3},{2,0},{3,1},{4,6},{5,7},{6,4},{7,5},{8,10},{9,11},{10,... | collective-permute-start | bytes 1597448 | tf_op jit(solution)/shard_map/ppermute | solution.py:572
  305.0 39.3 %collective-permute-start.33 = (bf16[1040,256]{1,0:T(8,128)(2,1)}, bf16[1040,256]{1,0:T(8,128)(2,1)}, u32[]{:S(2)}, u32[]{:S(2)}) collective-permute-start(bf16[1040,256]{1,0:T(8,128)(2,1)} %get-tuple-element.98), channel_id=1, source_target_pairs={{0,2},{1,3},{2,0},{3,1},{4,6},{5,7},{6,4},{7,5},{8,10},{9,11},{10,... | collective-permute-start | bytes 1597448 | tf_op jit(solution)/shard_map/ppermute | solution.py:572
  307.4 43.6 %collective-permute-start.57 = (bf16[192,656]{1,0:T(8,128)(2,1)S(1)}, bf16[192,656]{1,0:T(8,128)(2,1)}, u32[]{:S(2)}, u32[]{:S(2)}) collective-permute-start(bf16[192,656]{1,0:T(8,128)(2,1)S(1)} %dynamic-slice_bitcast_fusion.5), channel_id=1, source_target_pairs={{0,16},{4,20},{8,24},{12,28},{16,0},{20,4},{24,8},{28,12},{1,17},{... | collective-permute-start | bytes 755720 | tf_op jit(solution)/shard_map/ppermute | solution.py:621
  310.3 46.4 %collective-permute-start.60 = (bf16[192,656]{1,0:T(8,128)(2,1)S(1)}, bf16[192,656]{1,0:T(8,128)(2,1)S(1)}, u32[]{:S(2)}, u32[]{:S(2)}) collective-permute-start(bf16[192,656]{1,0:T(8,128)(2,1)S(1)} %dynamic-slice_bitcast_fusion.4), channel_id=1, source_target_pairs={{0,16},{4,20},{8,24},{12,28},{16,0},{20,4},{24,8},{28,12},{1,17},{... | collective-permute-start | bytes 755720 | tf_op jit(solution)/shard_map/ppermute | solution.py:621
  351.0 41.9 %collective-permute-start.34 = (bf16[1024,256]{1,0:T(8,128)(2,1)}, bf16[1024,256]{1,0:T(8,128)(2,1)}, u32[]{:S(2)}, u32[]{:S(2)}) collective-permute-start(bf16[1024,256]{1,0:T(8,128)(2,1)} %get-tuple-element.100.refs_2_), channel_id=1, source_target_pairs={{0,1},{1,0},{2,3},{3,2},{4,5},{5,4},{6,7},{7,6},{8,9},{9,8},{10,11... | collective-permute-start | bytes 1572872 | tf_op jit(solution)/shard_map/ppermute | solution.py:572
  365.8 27.2 %collective-permute-start.36 = (bf16[1024,256]{1,0:T(8,128)(2,1)}, bf16[1024,256]{1,0:T(8,128)(2,1)S(1)}, u32[]{:S(2)}, u32[]{:S(2)}) collective-permute-start(bf16[1024,256]{1,0:T(8,128)(2,1)} %collective-permute-done.35.refs_4_), channel_id=1, source_target_pairs={{0,1},{1,0},{2,3},{3,2},{4,5},{5,4},{6,7},{7,6},{8,9},{9,8},{10,11... | collective-permute-start | bytes 1572872 | tf_op jit(solution)/shard_map/ppermute | solution.py:572
  456.5 35.6 %collective-permute-start.54 = (bf16[256,256]{0,1:T(8,128)(2,1)S(1)}, bf16[256,256]{0,1:T(8,128)(2,1)S(1)}, u32[]{:S(2)}, u32[]{:S(2)}) collective-permute-start(bf16[256,256]{0,1:T(8,128)(2,1)S(1)} %dynamic-slice_bitcast_fusion.8), channel_id=1, source_target_pairs={{0,16},{4,20},{8,24},{12,28},{16,0},{20,4},{24,8},{28,12},{1,17},{... | collective-permute-start | bytes 393224 | tf_op jit(solution)/shard_map/ppermute | solution.py:621
  (58 other events, 683.5 us)
